TPU v7x, 32 devices: a whole 2x2x4 slice. The times are simulated.
32 devices in a mesh: slab: 8 (over y, x, core), blk: 4 (over z).
Axes of the slice: x: 2, y: 2, z: 4, core: 2. Of those that a mesh axis runs over, the one named last changes fastest.
Arguments:
- start_block: float32 [128, 64, 8, 128], P('blk', 'slab'), as said below
- locked_modes: float32 [384, 64, 8, 128], P('blk', 'slab'), as said below
- material: int32 [64, 8, 128], P('slab'), may hold values 0 or 1
- support: int32 [8, 128], replicated, may hold values 0 or 1
Outputs:
- basis: float32 [128, 64, 8, 128], P('blk', 'slab')
Inputs may be any that keep to these rules, and one draw needn't show every extreme that they name: `start_block`: A block of random vectors with large parts along the locked modes. `locked_modes`: each locked mode (one row) has about unit norm over all voxels.
All inputs are finite; a program needn't handle non-finite values. No bound on the sum of `material` on one device may be relied on, other than what follows from the above.
Results may differ from a plain program's by a relative error of at most 0.00014.
Values sent between devices are 32-bit elements; how exact they have to be, the bound alone decides.
No kernel may reach another device: no remote copies, remote signals or barrier semaphores. Data moves between devices by JAX's collectives and lax.ppermute only.
A program may use at most 64 MiB of HBM per device.

v0:
```python
import jax
import jax.numpy as jnp
from jax import lax
from jax.sharding import PartitionSpec as P

DEGREE = 8


THETA_LOAD = 0.1
VOID_ROOT = 0.31622776601683794
FILTER_CENTRE = 9.0
FILTER_HALF = 7.5


def padded_2(cells, sides, width):
    for axis, dim in sides:
        count = lax.axis_size(axis)
        ends = count - 1
        head = lax.slice_in_dim(cells, 0, width, axis=dim)
        tail = lax.slice_in_dim(cells, cells.shape[dim] - width, cells.shape[dim], axis=dim)
        cells = jnp.concatenate(
            [
                lax.ppermute(tail, axis, [(i, (i + 1) % count) for i in range(ends)]),
                cells,
                lax.ppermute(head, axis, [((i + 1) % count, i) for i in range(ends)]),
            ],
            axis=dim,
        )
    return cells


def blurred(padded):
    along_z = 0.5 * padded[:, :-2] + padded[:, 1:-1] + 0.5 * padded[:, 2:]
    along_y = 0.5 * along_z[:, :, :-2] + along_z[:, :, 1:-1] + 0.5 * along_z[:, :, 2:]
    along_x = 0.5 * along_y[..., :-2] + along_y[..., 1:-1] + 0.5 * along_y[..., 2:]
    return 2.0 * along_x


def operate(field, free_cells, root_stiff):
    kept_field = free_cells * field
    weighted = root_stiff * kept_field
    extended = padded_2(weighted, (("slab", 1),), 1)
    padded = jnp.pad(extended, ((0, 0), (0, 0), (1, 1), (1, 1)))
    smooth = blurred(padded)
    neighbours = padded[:, 2:, 1:-1, 1:-1] + padded[:, :-2, 1:-1, 1:-1]
    elastic = root_stiff * (16.0 * weighted - smooth)
    geometric = THETA_LOAD * root_stiff * (2.0 * weighted - neighbours)
    return free_cells * (elastic - geometric + 0.5 * kept_field) + (1.0 - free_cells) * field


def lower_inverse(gram):
    lower_factor = jnp.linalg.cholesky(gram)
    identity = jnp.eye(gram.shape[0], dtype=jnp.float32)
    return jax.scipy.linalg.solve_triangular(lower_factor, identity, lower=True)


def per_device(start_block, locked_modes, material, support):
    depth = material.shape[0]
    root_stiff = jnp.where(material == 1, 1.0, VOID_ROOT).astype(jnp.float32)
    layer = lax.axis_index("slab") * depth + lax.broadcasted_iota(jnp.int32, material.shape, 0)
    clamped = jnp.where(layer == 0, support[None, :, :], 0)
    free_cells = (1 - clamped).astype(jnp.float32)
    previous = start_block
    current = (
        operate(start_block, free_cells, root_stiff) - FILTER_CENTRE * start_block
    ) / FILTER_HALF
    for order_index in range(DEGREE - 1):
        following = (
            2.0 * (operate(current, free_cells, root_stiff) - FILTER_CENTRE * current) / FILTER_HALF
            - previous
        )
        previous = current
        current = following
    own_count = start_block.shape[0]
    cells = depth * start_block.shape[2] * start_block.shape[3]
    total_cells = cells * lax.axis_size("slab")
    flat = current.reshape(own_count, cells)
    modes_flat = locked_modes.reshape(locked_modes.shape[0], cells)
    gathered = lax.all_gather(flat, "blk", axis=0, tiled=True)
    correlations = lax.psum(
        jnp.dot(
            modes_flat,
            gathered.T,
            precision=lax.Precision.HIGHEST,
            preferred_element_type=jnp.float32,
        ),
        "slab",
    )
    own_deflated = flat - lax.psum_scatter(
        jnp.dot(
            correlations.T,
            modes_flat,
            precision=lax.Precision.HIGHEST,
            preferred_element_type=jnp.float32,
        ),
        "blk",
        scatter_dimension=0,
        tiled=True,
    )
    deflated = lax.all_gather(own_deflated, "blk", axis=0, tiled=True)
    gram = lax.psum(
        jnp.dot(
            deflated,
            deflated.T,
            precision=lax.Precision.HIGHEST,
            preferred_element_type=jnp.float32,
        ),
        "slab",
    )
    inverse = lower_inverse(gram)
    own_rows = lax.dynamic_slice_in_dim(inverse, lax.axis_index("blk") * own_count, own_count, 0)
    basis = jnp.sqrt(jnp.float32(total_cells)) * jnp.dot(
        own_rows, deflated, precision=lax.Precision.HIGHEST, preferred_element_type=jnp.float32
    )
    return basis.reshape(start_block.shape)


def solution(mesh):
    in_specs = (
        P("blk", "slab", None, None),
        P("blk", "slab", None, None),
        P("slab", None, None),
        P(),
    )
    out_specs = P("blk", "slab", None, None)
    return jax.shard_map(
        per_device, mesh=mesh, in_specs=in_specs, out_specs=out_specs, check_vma=False
    )
```

profile of v0, /device:TPU:0, one launch (start us, length us, event | category | flops | bytes accessed | tf_op | source)
XLA Modules:
  0.0 503.1 jit_solution(1023885015626496293)
XLA Ops:
  8.1 1.3 multiply_multiply_fusion.7
  9.5 1.3 collective-permute-start.1
  10.8 3.0 collective-permute-start
  14.8 2.2 select_maximum_fusion.14
  21.6 6.1 %collective-permute-start.2 = (f32[32,1,8,128]{3,2,1,0:T(8,128)S(1)}, f32[32,1,8,128]{3,2,1,0:T(8,128)S(1)}, u32[]{:S(2)}, u32[]{:S(2)}) collective-permute-start(f32[32,1,8,128]{3,2,1,0:T(8,128)S(1)} %get-tuple-element.32), channel_id=1, source_target_pairs={{0,4},{4,8},{8,12},{12,16},{16,20},{20,24},{24,28},{1,5},{5,9},{9,... | collective-permute-start | bytes 393224 | tf_op jit(solution)/shard_map/ppermute | solution.py:23
  28.7 2.2 select_maximum_fusion.12
  34.9 6.4 %collective-permute-start.4 = (f32[32,1,8,128]{3,2,1,0:T(8,128)S(1)}, f32[32,1,8,128]{3,2,1,0:T(8,128)S(1)}, u32[]{:S(2)}, u32[]{:S(2)}) collective-permute-start(f32[32,1,8,128]{3,2,1,0:T(8,128)S(1)} %get-tuple-element.30), channel_id=1, source_target_pairs={{0,4},{4,8},{8,12},{12,16},{16,20},{20,24},{24,28},{1,5},{5,9},{9,... | collective-permute-start | bytes 393224 | tf_op jit(solution)/shard_map/ppermute | solution.py:23
  41.8 2.2 select_maximum_fusion.10
  48.1 5.9 %collective-permute-start.6 = (f32[32,1,8,128]{3,2,1,0:T(8,128)S(1)}, f32[32,1,8,128]{3,2,1,0:T(8,128)S(1)}, u32[]{:S(2)}, u32[]{:S(2)}) collective-permute-start(f32[32,1,8,128]{3,2,1,0:T(8,128)S(1)} %get-tuple-element.28), channel_id=1, source_target_pairs={{0,4},{4,8},{8,12},{12,16},{16,20},{20,24},{24,28},{1,5},{5,9},{9,... | collective-permute-start | bytes 393224 | tf_op jit(solution)/shard_map/ppermute | solution.py:23
  55.0 2.2 select_maximum_fusion.8
  60.0 1.3 collective-permute-start.9
  61.3 5.9 %collective-permute-start.8 = (f32[32,1,8,128]{3,2,1,0:T(8,128)S(1)}, f32[32,1,8,128]{3,2,1,0:T(8,128)S(1)}, u32[]{:S(2)}, u32[]{:S(2)}) collective-permute-start(f32[32,1,8,128]{3,2,1,0:T(8,128)S(1)} %get-tuple-element.26), channel_id=1, source_target_pairs={{0,4},{4,8},{8,12},{12,16},{16,20},{20,24},{24,28},{1,5},{5,9},{9,... | collective-permute-start | bytes 393224 | tf_op jit(solution)/shard_map/ppermute | solution.py:23
  68.2 2.2 select_maximum_fusion.6
  74.4 6.1 %collective-permute-start.10 = (f32[32,1,8,128]{3,2,1,0:T(8,128)S(1)}, f32[32,1,8,128]{3,2,1,0:T(8,128)S(1)}, u32[]{:S(2)}, u32[]{:S(2)}) collective-permute-start(f32[32,1,8,128]{3,2,1,0:T(8,128)S(1)} %get-tuple-element.24), channel_id=1, source_target_pairs={{0,4},{4,8},{8,12},{12,16},{16,20},{20,24},{24,28},{1,5},{5,9},{9,... | collective-permute-start | bytes 393224 | tf_op jit(solution)/shard_map/ppermute | solution.py:23
  81.4 2.2 select_maximum_fusion.4
  87.6 5.9 %collective-permute-start.12 = (f32[32,1,8,128]{3,2,1,0:T(8,128)S(1)}, f32[32,1,8,128]{3,2,1,0:T(8,128)S(1)}, u32[]{:S(2)}, u32[]{:S(2)}) collective-permute-start(f32[32,1,8,128]{3,2,1,0:T(8,128)S(1)} %get-tuple-element.22), channel_id=1, source_target_pairs={{0,4},{4,8},{8,12},{12,16},{16,20},{20,24},{24,28},{1,5},{5,9},{9,... | collective-permute-start | bytes 393224 | tf_op jit(solution)/shard_map/ppermute | solution.py:23
  94.5 2.2 select_maximum_fusion.2
  100.8 6.4 %collective-permute-start.14 = (f32[32,1,8,128]{3,2,1,0:T(8,128)S(1)}, f32[32,1,8,128]{3,2,1,0:T(8,128)S(1)}, u32[]{:S(2)}, u32[]{:S(2)}) collective-permute-start(f32[32,1,8,128]{3,2,1,0:T(8,128)S(1)} %get-tuple-element.20), channel_id=1, source_target_pairs={{0,4},{4,8},{8,12},{12,16},{16,20},{20,24},{24,28},{1,5},{5,9},{9,... | collective-permute-start | bytes 393224 | tf_op jit(solution)/shard_map/ppermute | solution.py:23
  107.9 2.2 select_maximum_fusion
  113.8 1.6 copy.24
  115.5 93.3 %all-gather.3.cloned.1.call-done = f32[128,8192]{1,0:T(8,128)} async-done(((f32[32,8192]{1,0:T(8,128)}), f32[128,8192]{1,0:T(8,128)}) %all-gather.3.cloned.1.call-update) | async-done | bytes 4194320 | tf_op jit(solution)/shard_map/all_gather | solution.py:79
  208.7 7.6 %fusion.26 = f32[96,128]{0,1:T(8,128)S(1)} fusion(f32[128,8192]{1,0:T(8,128)} %all-gather.3.cloned.1.call-done, f32[12,8,64,128]{3,2,1,0:T(8,128)S(1)} %bitcast.36), kind=kOutput, calls=%fused_computation.95 | convolution fusion | flops 1207959552 | bytes 7389184 | tf_op jit(solution)/shard_map/dot_general | solution.py:81
  216.4 24.3 %psum.14 = f32[96,128]{0,1:T(8,128)S(1)} all-reduce(f32[96,128]{0,1:T(8,128)S(1)} %fusion.26), channel_id=1, replica_groups=mesh['slab'=8,'blk'=4] {'slab'}, use_global_device_ids=true, to_apply=%region_0.1 | all-reduce | flops 12288 | bytes 98304 | tf_op jit(solution)/shard_map/psum | solution.py:80
  240.7 7.9 %fusion.11 = f32[128,8192]{1,0:T(8,128)} fusion(f32[96,128]{0,1:T(8,128)S(1)} %psum.14, f32[12,8,64,128]{3,2,1,0:T(8,128)S(1)} %bitcast.37), kind=kOutput, calls=%fused_computation.56 | convolution fusion | flops 1207959552 | bytes 7389184 | tf_op jit(solution)/shard_map/dot_general | solution.py:90
  248.6 73.8 %reduce-scatter.2.cloned.1.call-done = f32[32,8192]{1,0:T(8,128)} async-done(((f32[128,8192]{1,0:T(8,128)}), f32[32,8192]{1,0:T(8,128)}) %reduce-scatter.2.cloned.1.call-update) | async-done | bytes 1048592 | tf_op jit(solution)/shard_map/reduce_scatter | solution.py:89
  322.4 2.8 fusion.147
  325.5 81.1 %all-gather.5.cloned.1.call-done = f32[128,8192]{1,0:T(8,128)} async-done(((f32[32,8192]{1,0:T(8,128)}), f32[128,8192]{1,0:T(8,128)}) %all-gather.5.cloned.1.call-update) | async-done | bytes 4194320 | tf_op jit(solution)/shard_map/all_gather | solution.py:100
  406.6 7.6 %fusion.163 = f32[128,128]{0,1:T(8,128)} fusion(f32[128,8192]{1,0:T(8,128)} %all-gather.5.cloned.1.call-done), kind=kOutput, calls=%fused_computation.283 | convolution fusion | flops 1610612736 | bytes 4259840 | tf_op jit(solution)/shard_map/dot_general | solution.py:102
  414.2 51.8 %all-reduce.10.cloned.1.call-done = f32[128,128]{0,1:T(8,128)} async-done(((f32[128,128]{0,1:T(8,128)}), f32[128,128]{0,1:T(8,128)}) %all-reduce.10.cloned.1.call-update) | async-done | bytes 65552 | tf_op jit(solution)/shard_map/psum | solution.py:101
  467.8 11.7 %cholesky.17 = f32[128,128]{1,0:T(8,128)S(1)} custom-call(f32[128,128]{1,0:T(8,128)S(1)} %fusion.142), custom_call_target="Cholesky" | custom-call | tf_op jit(solution)/shard_map/jit(cholesky)/cholesky | solution.py:52
  480.9 9.8 %custom-call.7 = f32[1,128,128]{1,2,0:T(8,128)S(1)} custom-call(f32[1,128,128]{2,1,0:T(8,128)S(1)} %fusion.139), custom_call_target="InvertDiagBlocksLowerTriangular" | custom-call | tf_op jit(solution)/shard_map/jit(_solve_triangular)/triangular_solve | solution.py:54
  491.0 4.0 fusion.25
  (81 shorter events, 43.9 us)
Async XLA Ops:
  6.5 202.2 %all-gather.3.cloned.1.call-start = ((), (), s32[]{:S(2)}) async-start(), calls=%async_computation.1 | async-start | bytes 5242880 | tf_op jit(solution)/shard_map/all_gather | solution.py:79
  9.5 5.1 %collective-permute-start.1 = (f32[32,1,8,128]{3,2,1,0:T(8,128)S(1)}, f32[32,1,8,128]{3,2,1,0:T(8,128)S(1)}, u32[]{:S(2)}, u32[]{:S(2)}) collective-permute-start(f32[32,1,8,128]{3,2,1,0:T(8,128)S(1)} %get-tuple-element.33), channel_id=1, source_target_pairs={{4,0},{8,4},{12,8},{16,12},{20,16},{24,20},{28,24},{5,1},{9,5},{13... | collective-permute-start | bytes 393224 | tf_op jit(solution)/shard_map/ppermute | solution.py:25
  10.8 4.0 collective-permute-start
  18.0 1.2 copy-start.1
  20.3 7.4 %collective-permute-start.3 = (f32[32,1,8,128]{3,2,1,0:T(8,128)S(1)}, f32[32,1,8,128]{3,2,1,0:T(8,128)S(1)}, u32[]{:S(2)}, u32[]{:S(2)}) collective-permute-start(f32[32,1,8,128]{3,2,1,0:T(8,128)S(1)} %get-tuple-element.31), channel_id=1, source_target_pairs={{4,0},{8,4},{12,8},{16,12},{20,16},{24,20},{28,24},{5,1},{9,5},{13... | collective-permute-start | bytes 393224 | tf_op jit(solution)/shard_map/ppermute | solution.py:25
  21.6 7.1 %collective-permute-start.2 = (f32[32,1,8,128]{3,2,1,0:T(8,128)S(1)}, f32[32,1,8,128]{3,2,1,0:T(8,128)S(1)}, u32[]{:S(2)}, u32[]{:S(2)}) collective-permute-start(f32[32,1,8,128]{3,2,1,0:T(8,128)S(1)} %get-tuple-element.32), channel_id=1, source_target_pairs={{0,4},{4,8},{8,12},{12,16},{16,20},{20,24},{24,28},{1,5},{5,9},{9,... | collective-permute-start | bytes 393224 | tf_op jit(solution)/shard_map/ppermute | solution.py:23
  33.6 7.7 %collective-permute-start.5 = (f32[32,1,8,128]{3,2,1,0:T(8,128)S(1)}, f32[32,1,8,128]{3,2,1,0:T(8,128)S(1)}, u32[]{:S(2)}, u32[]{:S(2)}) collective-permute-start(f32[32,1,8,128]{3,2,1,0:T(8,128)S(1)} %get-tuple-element.29), channel_id=1, source_target_pairs={{4,0},{8,4},{12,8},{16,12},{20,16},{24,20},{28,24},{5,1},{9,5},{13... | collective-permute-start | bytes 393224 | tf_op jit(solution)/shard_map/ppermute | solution.py:25
  34.9 6.9 %collective-permute-start.4 = (f32[32,1,8,128]{3,2,1,0:T(8,128)S(1)}, f32[32,1,8,128]{3,2,1,0:T(8,128)S(1)}, u32[]{:S(2)}, u32[]{:S(2)}) collective-permute-start(f32[32,1,8,128]{3,2,1,0:T(8,128)S(1)} %get-tuple-element.30), channel_id=1, source_target_pairs={{0,4},{4,8},{8,12},{12,16},{16,20},{20,24},{24,28},{1,5},{5,9},{9,... | collective-permute-start | bytes 393224 | tf_op jit(solution)/shard_map/ppermute | solution.py:23
  46.8 7.3 %collective-permute-start.7 = (f32[32,1,8,128]{3,2,1,0:T(8,128)S(1)}, f32[32,1,8,128]{3,2,1,0:T(8,128)S(1)}, u32[]{:S(2)}, u32[]{:S(2)}) collective-permute-start(f32[32,1,8,128]{3,2,1,0:T(8,128)S(1)} %get-tuple-element.27), channel_id=1, source_target_pairs={{4,0},{8,4},{12,8},{16,12},{20,16},{24,20},{28,24},{5,1},{9,5},{13... | collective-permute-start | bytes 393224 | tf_op jit(solution)/shard_map/ppermute | solution.py:25
  48.1 6.9 %collective-permute-start.6 = (f32[32,1,8,128]{3,2,1,0:T(8,128)S(1)}, f32[32,1,8,128]{3,2,1,0:T(8,128)S(1)}, u32[]{:S(2)}, u32[]{:S(2)}) collective-permute-start(f32[32,1,8,128]{3,2,1,0:T(8,128)S(1)} %get-tuple-element.28), channel_id=1, source_target_pairs={{0,4},{4,8},{8,12},{12,16},{16,20},{20,24},{24,28},{1,5},{5,9},{9,... | collective-permute-start | bytes 393224 | tf_op jit(solution)/shard_map/ppermute | solution.py:23
  60.0 7.3 %collective-permute-start.9 = (f32[32,1,8,128]{3,2,1,0:T(8,128)S(1)}, f32[32,1,8,128]{3,2,1,0:T(8,128)S(1)}, u32[]{:S(2)}, u32[]{:S(2)}) collective-permute-start(f32[32,1,8,128]{3,2,1,0:T(8,128)S(1)} %get-tuple-element.25), channel_id=1, source_target_pairs={{4,0},{8,4},{12,8},{16,12},{20,16},{24,20},{28,24},{5,1},{9,5},{13... | collective-permute-start | bytes 393224 | tf_op jit(solution)/shard_map/ppermute | solution.py:25
  61.3 6.9 %collective-permute-start.8 = (f32[32,1,8,128]{3,2,1,0:T(8,128)S(1)}, f32[32,1,8,128]{3,2,1,0:T(8,128)S(1)}, u32[]{:S(2)}, u32[]{:S(2)}) collective-permute-start(f32[32,1,8,128]{3,2,1,0:T(8,128)S(1)} %get-tuple-element.26), channel_id=1, source_target_pairs={{0,4},{4,8},{8,12},{12,16},{16,20},{20,24},{24,28},{1,5},{5,9},{9,... | collective-permute-start | bytes 393224 | tf_op jit(solution)/shard_map/ppermute | solution.py:23
  73.1 7.4 %collective-permute-start.11 = (f32[32,1,8,128]{3,2,1,0:T(8,128)S(1)}, f32[32,1,8,128]{3,2,1,0:T(8,128)S(1)}, u32[]{:S(2)}, u32[]{:S(2)}) collective-permute-start(f32[32,1,8,128]{3,2,1,0:T(8,128)S(1)} %get-tuple-element.23), channel_id=1, source_target_pairs={{4,0},{8,4},{12,8},{16,12},{20,16},{24,20},{28,24},{5,1},{9,5},{13... | collective-permute-start | bytes 393224 | tf_op jit(solution)/shard_map/ppermute | solution.py:25
  74.4 6.9 %collective-permute-start.10 = (f32[32,1,8,128]{3,2,1,0:T(8,128)S(1)}, f32[32,1,8,128]{3,2,1,0:T(8,128)S(1)}, u32[]{:S(2)}, u32[]{:S(2)}) collective-permute-start(f32[32,1,8,128]{3,2,1,0:T(8,128)S(1)} %get-tuple-element.24), channel_id=1, source_target_pairs={{0,4},{4,8},{8,12},{12,16},{16,20},{20,24},{24,28},{1,5},{5,9},{9,... | collective-permute-start | bytes 393224 | tf_op jit(solution)/shard_map/ppermute | solution.py:23
  86.3 7.3 %collective-permute-start.13 = (f32[32,1,8,128]{3,2,1,0:T(8,128)S(1)}, f32[32,1,8,128]{3,2,1,0:T(8,128)S(1)}, u32[]{:S(2)}, u32[]{:S(2)}) collective-permute-start(f32[32,1,8,128]{3,2,1,0:T(8,128)S(1)} %get-tuple-element.21), channel_id=1, source_target_pairs={{4,0},{8,4},{12,8},{16,12},{20,16},{24,20},{28,24},{5,1},{9,5},{13... | collective-permute-start | bytes 393224 | tf_op jit(solution)/shard_map/ppermute | solution.py:25
  87.6 6.9 %collective-permute-start.12 = (f32[32,1,8,128]{3,2,1,0:T(8,128)S(1)}, f32[32,1,8,128]{3,2,1,0:T(8,128)S(1)}, u32[]{:S(2)}, u32[]{:S(2)}) collective-permute-start(f32[32,1,8,128]{3,2,1,0:T(8,128)S(1)} %get-tuple-element.22), channel_id=1, source_target_pairs={{0,4},{4,8},{8,12},{12,16},{16,20},{20,24},{24,28},{1,5},{5,9},{9,... | collective-permute-start | bytes 393224 | tf_op jit(solution)/shard_map/ppermute | solution.py:23
  99.5 7.7 %collective-permute-start.15 = (f32[32,1,8,128]{3,2,1,0:T(8,128)S(1)}, f32[32,1,8,128]{3,2,1,0:T(8,128)S(1)}, u32[]{:S(2)}, u32[]{:S(2)}) collective-permute-start(f32[32,1,8,128]{3,2,1,0:T(8,128)S(1)} %get-tuple-element.19), channel_id=1, source_target_pairs={{4,0},{8,4},{12,8},{16,12},{20,16},{24,20},{28,24},{5,1},{9,5},{13... | collective-permute-start | bytes 393224 | tf_op jit(solution)/shard_map/ppermute | solution.py:25
  100.8 7.1 %collective-permute-start.14 = (f32[32,1,8,128]{3,2,1,0:T(8,128)S(1)}, f32[32,1,8,128]{3,2,1,0:T(8,128)S(1)}, u32[]{:S(2)}, u32[]{:S(2)}) collective-permute-start(f32[32,1,8,128]{3,2,1,0:T(8,128)S(1)} %get-tuple-element.20), channel_id=1, source_target_pairs={{0,4},{4,8},{8,12},{12,16},{16,20},{20,24},{24,28},{1,5},{5,9},{9,... | collective-permute-start | bytes 393224 | tf_op jit(solution)/shard_map/ppermute | solution.py:23
  111.7 97.0 %copy-start = (f32[96,8,8,128]{3,2,1,0:T(8,128)S(1)}, f32[96,8,8,128]{3,2,1,0:T(8,128)}, u32[]{:S(2)}) copy-start(f32[96,8,8,128]{3,2,1,0:T(8,128)} %param.5) | copy-start | bytes 9437188
  112.8 1.0 copy-start.2
  115.4 207.0 %reduce-scatter.2.cloned.1.call-start = ((), (), s32[]{:S(2)}) async-start(), calls=%async_computation.2 | async-start | bytes 5242880 | tf_op jit(solution)/shard_map/reduce_scatter | solution.py:89
  248.5 73.8 %copy-start.3 = (f32[32,8,8,128]{3,2,1,0:T(8,128)S(1)}, f32[32,8,8,128]{3,2,1,0:T(8,128)}, u32[]{:S(2)}) copy-start(f32[32,8,8,128]{3,2,1,0:T(8,128)} %copy-done.2) | copy-start | bytes 3145732
  248.6 158.1 %all-gather.5.cloned.1.call-start = ((), (), s32[]{:S(2)}) async-start(), calls=%async_computation.3 | async-start | bytes 5242880 | tf_op jit(solution)/shard_map/all_gather | solution.py:100
  325.2 140.8 %all-reduce.10.cloned.1.call-start = ((), (), s32[]{:S(2)}) async-start(), calls=%async_computation.4 | async-start | bytes 131072 | tf_op jit(solution)/shard_map/psum | solution.py:101
Sparse Core Ops, SparseCore 0:
  115.5 93.1 all-gather.2
  248.7 73.6 reduce-scatter.1
  325.3 81.2 all-gather.4
  414.4 51.6 all-reduce.9
where the time goes:
time: 510 us; the launch traced here: 503 us
  waiting for transfers between devices  306 us (60%)
  other arithmetic  69.2 us (14%)
  starting transfers between devices  56.6 us (11%)
  matrix products  27.3 us (5%)
  blocking collectives  24.3 us (5%)
  between operations  14.2 us (3%)
  local copies, waits for them, and re-layouts  5.53 us (1%)
    all_gather x1, waiting for transfers between devices, per_device(): gathered = lax.all_gather(flat, 'blk', axis=0, tiled=True)  93.3 us
    all_gather x1, waiting for transfers between devices, per_device(): deflated = lax.all_gather(own_deflated, 'blk', axis=0, tiled=True)  81.1 us
    reduce_scatter x1, waiting for transfers between devices, per_device(): lax.psum_scatter(jnp.dot(correlations.T, modes_flat, precision=lax.Precis...  73.8 us
    psum x1, waiting for transfers between devices, per_device(): lax.psum(jnp.dot(deflated, deflated.T, precision=lax.Precision.HIGHEST, p...  51.8 us
    ppermute x8, starting transfers between devices, padded_2(): lax.ppermute(tail, axis, [(i, (i + 1) % count) for i in range(ends)])  45.9 us
    psum x1, blocking collectives, per_device(): lax.psum(jnp.dot(modes_flat, gathered.T, precision=lax.Precision.HIGHEST,...  24.3 us
    concatenate x8, other arithmetic, padded_2(): jnp.concatenate([lax.ppermute(tail, axis, [(i, (i + 1) % count) for i in...  18 us
    another operation x3, other arithmetic, lower_inverse(): lower_factor = jnp.linalg.cholesky(gram)  12.4 us
  transfers between devices with their start and end apart: 20, of which 12 were waited for; matrix products, arithmetic and copies ran while one was open for 0% of the time, Pallas kernels for 0%

commit v1 on v0

v1 whole, which is shorter than its diff:
```python
import jax
import jax.numpy as jnp
from jax import lax
from jax.experimental import pallas as pl
from jax.experimental.pallas import tpu as pltpu
from jax.sharding import PartitionSpec as P

DEGREE = 8
THETA_LOAD = 0.1
VOID_ROOT = 0.31622776601683794
FILTER_CENTRE = 9.0
FILTER_HALF = 7.5


HIGHEST = lax.Precision.HIGHEST
F32 = jnp.float32
TILE = 8


def swap(x, axis, bits):
    return lax.ppermute(x, axis, [(i, i ^ bits) for i in range(lax.axis_size(axis))])


def whole(shape):
    return pl.BlockSpec(shape, lambda *_: (0,) * len(shape))


def smem():
    return pl.BlockSpec(memory_space=pltpu.SMEM)


def call(kernel, place, args, outs, scratch=()):
    return pl.pallas_call(
        kernel,
        in_specs=[smem()] + [whole(a.shape) for a in args],
        out_specs=[whole(s) for s in outs],
        out_shape=[jax.ShapeDtypeStruct(s, F32) for s in outs],
        scratch_shapes=[pltpu.VMEM(s, F32) for s in scratch],
    )(place, *args)


def dot(a, b, da, db):
    return lax.dot_general(
        a, b, (((da,), (db,)), ((), ())), precision=HIGHEST, preferred_element_type=F32
    )


def in_line(ref):
    return jnp.concatenate([ref[r] for r in range(ref.shape[0])], axis=1)


def near_kernel(place, modes, *outs, total):
    count = modes.shape[0] // total
    share = outs[0].shape[0]
    for k, out in enumerate(outs):
        start = (place[0] ^ (k + 1)) * share
        for i in range(share):
            out[i] = modes[pl.ds(start + i, count, stride=total), :]


def far_kernel(place, modes, near, far, *outs, total):
    count = modes.shape[0] // total
    share = near.shape[0]
    start = place[0] * share
    for i in range(share):
        near[i] = modes[pl.ds(start + i, count, stride=total), :]
    first = total - far.shape[0]
    for i in range(far.shape[0]):
        far[i] = modes[pl.ds(first + i, count, stride=total), :]
    share = outs[0].shape[0]
    for k, out in enumerate(outs):
        start = first + (place[0] ^ k) * share
        for i in range(share):
            out[i] = modes[pl.ds(start + i, count, stride=total), :]


def split_modes(kernel, place, modes, outs, block):
    total = modes.shape[0] // outs[0][1]
    nx = modes.shape[1]
    return pl.pallas_call(
        lambda *refs: kernel(*refs, total=total),
        grid=(outs[0][1] // block,),
        in_specs=[smem(), pl.BlockSpec((block * total, nx), lambda g: (g, 0))],
        out_specs=[pl.BlockSpec((s[0], block, nx), lambda g: (0, g, 0)) for s in outs],
        out_shape=[jax.ShapeDtypeStruct(s, F32) for s in outs],
    )(place, modes)


def filter_kernel(place, own, below, above, coef_own, coef_below, coef_above, clamped, *rest, steps, ny):
    outs, (one, two, square, mixed, back) = rest[:-5], rest[-5:]
    nx = own.shape[1]
    depth = coef_own.shape[0]
    halo = coef_below.shape[0]
    total = depth + 2 * halo
    scale = 2.0 / FILTER_HALF
    col = lax.broadcasted_iota(jnp.int32, (TILE, nx), 1)
    left = jnp.where(col > 0, 0.5, 0.0).astype(F32)
    right = jnp.where(col < nx - 1, 0.5, 0.0).astype(F32)
    bulk = F32(scale * (0.5 - FILTER_CENTRE))
    near = F32(THETA_LOAD)
    centre = F32(16.0 - 4.0 * THETA_LOAD)

    @pl.when(pl.program_id(0) == 0)
    def _():
        for i in range(total):
            if i < halo:
                coef = coef_below[i]
            elif i < halo + depth:
                coef = coef_own[i - halo]
            else:
                coef = coef_above[i - halo - depth]
            for y in range(ny):
                row = jnp.broadcast_to(coef[y : y + 1, :], (TILE, nx))
                weight = F32(scale) * row * row
                square[i, y] = weight
                mixed[i, y] = centre * weight + bulk
                if halo <= i < halo + depth:
                    back[i - halo, y] = jnp.where(row > 0, 1.0 / jnp.where(row > 0, row, 1.0), 0.0)

    for i in range(total):
        if i < halo:
            source, base, layers, coef = below, i, halo, coef_below[i]
        elif i < halo + depth:
            source, base, layers, coef = own, i - halo, depth, coef_own[i - halo]
        else:
            source, base, layers, coef = above, i - halo - depth, halo, coef_above[i - halo - depth]
        for y in range(ny):
            value = source[pl.ds(base * ny + y, TILE, stride=layers * ny), :]
            one[i, y] = jnp.broadcast_to(coef[y : y + 1, :], (TILE, nx)) * value

    current, previous = one, two
    for step in range(steps):
        lo, hi = step + 1, total - 1 - step

        def layer(i, carry, step=step, current=current, previous=previous):
            here, pair = carry
            after = [current[i + 1, y] for y in range(ny)]
            pair_after = [here[y] + after[y] for y in range(ny)]
            line = [pair[y] + pair_after[y] for y in range(ny)]
            across = [line[y] + line[y + 1] for y in range(ny - 1)]
            for y in range(ny):
                if y == 0:
                    plane = across[0] + line[0]
                elif y == ny - 1:
                    plane = across[y - 1] + line[y]
                else:
                    plane = across[y - 1] + across[y]
                cube = plane + left * pltpu.roll(plane, 1, 1) + right * pltpu.roll(plane, nx - 1, 1)
                new = mixed[i, y] * here[y] + square[i, y] * (near * line[y] - 0.5 * cube)
                if step == 0:
                    previous[i, y] = 0.5 * new
                else:
                    previous[i, y] = new - previous[i, y]
            return after, pair_after

        before = [current[lo - 1, y] for y in range(ny)]
        here = [current[lo, y] for y in range(ny)]
        carry = (here, [before[y] + here[y] for y in range(ny)])
        for i in range(lo, hi):
            carry = layer(i, carry)
        current, previous = previous, current

    before, now = 1.0, (1.0 - FILTER_CENTRE) / FILTER_HALF
    for _ in range(steps - 1):
        before, now = now, 2.0 * now * (1.0 - FILTER_CENTRE) / FILTER_HALF - before
    for i in range(depth):
        for y in range(ny):
            value = back[i, y] * current[halo + i, y]
            if i == 0:
                fixed = jnp.broadcast_to(clamped[y : y + 1, :], (TILE, nx))
                value = value + F32(now) * fixed * own[pl.ds(y, TILE, stride=depth * ny), :]
            previous[i, y] = value
    rows = previous.reshape(total * ny, TILE, nx)
    far = outs[-1]
    far[...] = rows[pl.ds(depth * ny - far.shape[0], far.shape[0])]
    for k, out in enumerate(outs[:-1]):
        out[...] = rows[pl.ds((place[0] ^ k) * out.shape[0], out.shape[0])]


def filtered_rows(place, start_block, coef_own, clamped, near_rows, far_rows, parts):
    count, depth, ny, nx = start_block.shape
    halo = DEGREE
    assert depth >= halo and count % TILE == 0
    slabs = lax.axis_size("slab")
    rise = [(i, i + 1) for i in range(slabs - 1)]
    fall = [(i + 1, i) for i in range(slabs - 1)]
    below = lax.ppermute(start_block[:, depth - halo :], "slab", rise)
    above = lax.ppermute(start_block[:, :halo], "slab", fall)
    coef_below = lax.ppermute(coef_own[depth - halo :], "slab", rise)
    coef_above = lax.ppermute(coef_own[:halo], "slab", fall)
    outs = [(near_rows // parts, count, nx)] * parts + [(far_rows, count, nx)]
    total = depth + 2 * halo
    got = pl.pallas_call(
        lambda *refs: filter_kernel(*refs, steps=DEGREE, ny=ny),
        grid=(count // TILE,),
        in_specs=[smem()]
        + [pl.BlockSpec((TILE * n * ny, nx), lambda g: (g, 0)) for n in (depth, halo, halo)]
        + [whole(c.shape) for c in (coef_own, coef_below, coef_above, clamped)],
        out_specs=[pl.BlockSpec((s[0], TILE, nx), lambda g: (0, g, 0)) for s in outs],
        out_shape=[jax.ShapeDtypeStruct(s, F32) for s in outs],
        scratch_shapes=[pltpu.VMEM((total, ny, TILE, nx), F32)] * 4 + [pltpu.VMEM((depth, ny, TILE, nx), F32)],
        name="chebyshev",
    )(
        place,
        start_block.reshape(-1, nx),
        below.reshape(-1, nx),
        above.reshape(-1, nx),
        coef_own,
        coef_below,
        coef_above,
        clamped,
    )
    return list(got[:-1]), got[-1]


def gather_fields(place, parts, fields):
    count = parts[0].shape[1]
    for k, part in enumerate(parts):
        start = pl.multiple_of((place[0] ^ k) * count, TILE)
        fields[:, pl.ds(start, count), :] = part[...]


def near_correlate_kernel(place, *refs, parts):
    modes, pieces, fields, outs = refs[:parts], refs[parts : 2 * parts], refs[2 * parts], refs[2 * parts + 1 :]
    gather_fields(place, pieces, fields)
    own = in_line(fields)
    stack = jnp.concatenate([in_line(m) for m in modes], axis=0)
    value = dot(stack, own, 1, 1)
    size = outs[0].shape[0]
    for k, out in enumerate(outs):
        out[...] = value[k * size : (k + 1) * size]


def far_correlate_kernel(place, modes, *refs, parts):
    pieces, sums, fields, out = refs[:parts], refs[parts : 2 * parts], refs[2 * parts], refs[2 * parts + 1]
    gather_fields(place, pieces, fields)
    value = dot(in_line(modes), in_line(fields), 1, 1)
    for s in sums:
        value = value + s[...]
    out[...] = value


def halves(core, value, mine, other):
    size = mine.shape[0]

    @pl.when(core == 0)
    def _():
        mine[...] = value[:size]
        other[...] = value[size:]

    @pl.when(core == 1)
    def _():
        mine[...] = value[size:]
        other[...] = value[:size]


def deflate_kernel(place, *refs, parts):
    corr, near, far = refs[:parts], refs[parts : 2 * parts], refs[2 * parts : 3 * parts]
    near_fields, far_fields, deflated, mine, other = refs[3 * parts :]
    share = far[0].shape[0]
    fields = [near_fields[r] for r in range(near_fields.shape[0])]
    fields += [far_fields[place[0] * share + r] for r in range(share)]
    modes = jnp.concatenate(
        [jnp.concatenate([in_line(a), in_line(b)], axis=1) for a, b in zip(near, far)], axis=0
    )
    stack = jnp.concatenate([c[...] for c in corr], axis=0)
    value = jnp.concatenate(fields, axis=1) - dot(stack, modes, 0, 0)
    deflated[...] = value
    halves(place[1], dot(value, value, 1, 1), mine, other)


def lower_inverse(aug, out, count):
    tile, block = TILE, min(64, count)
    row = lax.broadcasted_iota(jnp.int32, (tile, count), 0)
    for top in range(0, count, block):
        q = block // tile
        left = [aug[top + i * tile : top + (i + 1) * tile, :count] for i in range(q)]
        right = [aug[top + i * tile : top + (i + 1) * tile, count:] for i in range(q)]
        for i in range(q):
            first = top + i * tile
            cols = {
                j: [jnp.broadcast_to(left[j][:, first + s : first + s + 1], (tile, count)) for s in range(tile)]
                for j in range(i, q)
            }
            roots = jnp.zeros((tile, count), F32)
            for t in range(tile):
                pick = lambda x: jnp.broadcast_to(x[t : t + 1, :], (tile, count))
                pivot = pick(cols[i][t])
                roots = jnp.where(row == t, lax.rsqrt(pivot), roots)
                over = 1.0 / pivot
                heads = {s: pick(cols[i][s]) for s in range(t + 1, tile)}
                head_left, head_right = pick(left[i]), pick(right[i])
                for j in range(i, q):
                    factor = cols[j][t] * over
                    if j == i:
                        factor = jnp.where(row > t, factor, 0.0)
                    for s in range(t + 1, tile):
                        cols[j][s] = cols[j][s] - factor * heads[s]
                    left[j] = left[j] - factor * head_left
                    right[j] = right[j] - factor * head_right
            left[i] = left[i] * roots
            right[i] = right[i] * roots
            out[first : first + tile, :] = right[i]
        low = top + block
        if low < count:
            upper = jnp.concatenate(left, axis=0)
            lane = lax.broadcasted_iota(jnp.int32, upper.shape, 1)
            both = jnp.concatenate([upper, jnp.concatenate(right, axis=0)], axis=1)
            change = dot(jnp.where(lane >= low, upper, 0.0), both, 0, 0)
            aug[low:, :] = aug[low:, :] - change[low:, :]


def basis_kernel(place, mine, other, deflated, *rest, scale):
    outs, aug, inverse = rest[:-2], rest[-2], rest[-1]
    count = deflated.shape[0]
    half = mine.shape[0]

    @pl.when(place[1] == 0)
    def _():
        aug[:half, :count] = mine[...]
        aug[half:, :count] = other[...]

    @pl.when(place[1] == 1)
    def _():
        aug[half:, :count] = mine[...]
        aug[:half, :count] = other[...]

    r = lax.broadcasted_iota(jnp.int32, (count, count), 0)
    c = lax.broadcasted_iota(jnp.int32, (count, count), 1)
    aug[:, count:] = jnp.where(r == c, 1.0, 0.0).astype(F32)
    lower_inverse(aug, inverse, count)
    rows, size, nx = outs[0].shape
    order = [
        inverse[pl.ds(pl.multiple_of((place[0] ^ k) * size, TILE), size), :] for k in range(len(outs))
    ]
    value = dot(scale * jnp.concatenate(order, axis=0), deflated[...], 1, 0)
    for k, out in enumerate(outs):
        for i in range(rows):
            out[i] = value[k * size : (k + 1) * size, i * nx : (i + 1) * nx]


def place_kernel(place, *refs, near_share, far_share, near_rows):
    parts, out = refs[:-1], refs[-1]
    count, _ = parts[0].shape[1:]
    total = out.shape[0] // count
    for k, part in enumerate(parts):
        for i in range(near_share + far_share):
            if i < near_share:
                row = (place[0] ^ k) * near_share + i
            else:
                row = near_rows + (place[0] ^ k) * far_share + i - near_share
            out[pl.ds(row, count, stride=total), :] = part[i]


def groups_of(size, first):
    bits = []
    while first < size:
        bits.append(first)
        first *= 2
    out = []
    while bits:
        take, bits = bits[:2], bits[2:]
        out.append(take if len(take) == 1 else [take[0], take[1], take[0] | take[1]])
    return out


def summed(x, axis, first):
    for group in groups_of(lax.axis_size(axis), first):
        got = [swap(x, axis, bits) for bits in group]
        for g in got:
            x = x + g
    return x


def order_of(parts):
    far = [k for k in range(parts) if 2 * k >= parts]
    return far + [k for k in range(1, parts) if 2 * k < parts]


def per_device(start_block, locked_modes, material, support):
    depth, ny, nx = material.shape
    own_count, own_modes = start_block.shape[0], locked_modes.shape[0]
    parts = lax.axis_size("blk")
    slab, z = lax.axis_index("slab"), lax.axis_index("blk")
    place = jnp.stack([z, slab % 2]).astype(jnp.int32)
    rows = depth * ny
    far_share = max(1, rows // (4 * parts))
    far_rows = far_share * parts
    near_rows = rows - far_rows
    near_share = near_rows // parts
    count = own_count * parts
    ks = range(parts)
    order = order_of(parts)

    def exchanged(pieces):
        got = {k: swap(pieces[k], "blk", k) for k in order}
        return [got[k] if k else pieces[0] for k in ks]

    def gathered(piece):
        have, bit = {0: piece}, parts // 2
        while bit:
            got = {k ^ bit: swap(x, "blk", bit) for k, x in have.items()}
            have |= got
            bit //= 2
        return [have[k] for k in ks]

    modes = locked_modes.reshape(-1, nx)
    block = own_modes // 2 if own_modes % (2 * TILE) == 0 else own_modes
    near_modes = split_modes(
        near_kernel, place, modes, [(near_share, own_modes, nx)] * (parts - 1), block
    )
    start_block, *near_modes = lax.optimization_barrier([start_block] + list(near_modes))
    near_modes = exchanged([None] + near_modes)
    near_modes[0], far_own, *far_modes = split_modes(
        far_kernel,
        place,
        modes,
        [(near_share, own_modes, nx), (far_rows, own_modes, nx)] + [(far_share, own_modes, nx)] * parts,
        block,
    )

    root_stiff = jnp.where(material == 1, 1.0, VOID_ROOT).astype(F32)
    clamped = jnp.where(slab == 0, support, 0).astype(F32)
    layer = lax.broadcasted_iota(jnp.int32, material.shape, 0)
    coef_own = jnp.where(layer == 0, 1.0 - clamped[None], 1.0) * root_stiff
    near_fields, far_field = filtered_rows(
        place, start_block, coef_own, clamped, near_rows, far_rows, parts
    )
    near_fields = exchanged(near_fields)
    far_field, *near_fields = lax.optimization_barrier([far_field] + near_fields)
    far_fields = gathered(far_field)

    near_all, *sums = call(
        lambda *refs: near_correlate_kernel(*refs, parts=parts),
        place,
        near_modes + near_fields,
        [(near_share, count, nx)] + [(own_modes, count)] * parts,
    )
    sums = exchanged(sums)
    middle = parts // 2
    *far_modes, far_fields[middle] = lax.optimization_barrier(far_modes + [far_fields[middle]])
    far_modes = exchanged(far_modes)
    far_all, corr = call(
        lambda *refs: far_correlate_kernel(*refs, parts=parts),
        place,
        [far_own] + far_fields + sums,
        [(far_rows, count, nx), (own_modes, count)],
    )
    corr = corr + swap(corr, "slab", 1)
    corr = summed(corr, "slab", 2)
    corr = exchanged([corr] * parts)
    deflated, mine, other = call(
        lambda *refs: deflate_kernel(*refs, parts=parts),
        place,
        corr + near_modes + far_modes + [near_all, far_all],
        [(count, (near_share + far_share) * nx), (count // 2, count), (count // 2, count)],
    )
    gram = summed(summed(mine + swap(other, "slab", 1), "slab", 2), "blk", 1)
    total_cells = rows * nx * lax.axis_size("slab")
    scale = float(total_cells) ** 0.5
    outs = call(
        lambda *refs: basis_kernel(*refs, scale=scale),
        place,
        [gram, swap(gram, "slab", 1), deflated],
        [(near_share + far_share, own_count, nx)] * parts,
        scratch=[(count, 2 * count), (count, count)],
    )
    outs = exchanged(list(outs))
    (basis,) = call(
        lambda *refs: place_kernel(*refs, near_share=near_share, far_share=far_share, near_rows=near_rows),
        place,
        outs,
        [(own_count * rows, nx)],
    )
    return basis.reshape(start_block.shape)


def solution(mesh):
    in_specs = (
        P("blk", "slab", None, None),
        P("blk", "slab", None, None),
        P("slab", None, None),
        P(),
    )
    out_specs = P("blk", "slab", None, None)

    return jax.shard_map(
        per_device, mesh=mesh, in_specs=in_specs, out_specs=out_specs, check_vma=False
    )
```

time: 510 us -> 244 us (0.48)
  waiting for transfers between devices: 306 us -> 114 us
  other arithmetic: 69.2 us -> 2.88 us
  Pallas kernels: 0 us -> 44.4 us
  matrix products: 27.3 us -> 0 us
  blocking collectives: 24.3 us -> 0 us
  starting transfers between devices: 56.6 us -> 73.9 us
  between operations: 14.2 us -> 0.36 us
    all_gather x2 -> x0, waiting for transfers between devices: 174 us -> none  [the longest x1 93.3 us: per_device(): gathered = lax.all_gather(flat, 'blk', axis=0, tiled=True)]
    ppermute x16 -> x37, waiting for transfers between devices: 6 us -> 114 us  [the longest x33 113 us: swap(): lax.ppermute(x, axis, [(i, i ^ bits) for i in range(lax.axis_size(axis))])]
    reduce_scatter x1 -> x0, waiting for transfers between devices: 73.8 us -> none  [per_device(): lax.psum_scatter(jnp.dot(correlations.T, modes_flat, precision=lax.Precis...]
    psum x1 -> x0, waiting for transfers between devices: 51.8 us -> none  [per_device(): lax.psum(jnp.dot(deflated, deflated.T, precision=lax.Precision.HIGHEST, p...]
    pallas_call x0 -> x8, Pallas kernels: none -> 44.4 us  [the longest x5 24.7 us: call(): pl.pallas_call(kernel, in_specs=[smem()] + [whole(a.shape) for a in args]...]
    dot_general x4 -> x0, matrix products: 27.1 us -> none  [the longest x1 7.87 us: per_device(): jnp.dot(correlations.T, modes_flat, precision=lax.Precision.HIGHEST, pref...]
    psum x1 -> x0, blocking collectives: 24.3 us -> none  [per_device(): lax.psum(jnp.dot(modes_flat, gathered.T, precision=lax.Precision.HIGHEST,...]
    another operation x5 -> x1, other arithmetic: 22.9 us -> 0.59 us  [per_device(): place = jnp.stack([z, slab % 2]).astype(jnp.int32)]
  transfers between devices with their start and end apart: 20 -> 37, of which waited for: 12 -> 18; matrix products, arithmetic and copies ran while one was open for 0% -> 0% of each run, Pallas kernels for 0% -> 3%
where the time goes in v1:
time: 244 us; the launch traced here: 241 us
  waiting for transfers between devices  114 us (47%)
  starting transfers between devices  73.9 us (30%)
  Pallas kernels  44.4 us (18%)
  local copies, waits for them, and re-layouts  5.29 us (2%)
  other arithmetic  2.88 us (1%)
    ppermute x33, waiting for transfers between devices, swap(): lax.ppermute(x, axis, [(i, i ^ bits) for i in range(lax.axis_size(axis))])  113 us
    ppermute x33, starting transfers between devices, swap(): lax.ppermute(x, axis, [(i, i ^ bits) for i in range(lax.axis_size(axis))])  63.1 us
    pallas_call x5, Pallas kernels, call(): pl.pallas_call(kernel, in_specs=[smem()] + [whole(a.shape) for a in args]...  24.7 us
    pallas_call x1, Pallas kernels, filtered_rows(): pl.pallas_call(lambda *refs: filter_kernel(*refs, steps=DEGREE, ny=ny), g...  12.4 us
    pallas_call x2, Pallas kernels, split_modes(): pl.pallas_call(lambda *refs: kernel(*refs, total=total), grid=(outs[0][1]...  7.35 us
    unnamed x68, local copies, waits for them, and re-layouts  5.29 us
    ppermute x1, starting transfers between devices, filtered_rows(): coef_below = lax.ppermute(coef_own[depth - halo:], 'slab', rise)  5.06 us
  transfers between devices with their start and end apart: 37, of which 18 were waited for; matrix products, arithmetic and copies ran while one was open for 0% of the time, Pallas kernels for 3%

profile of v1, /device:TPU:0, one launch (start us, length us, event | category | flops | bytes accessed | tf_op | source)
XLA Modules:
  0.0 241.1 jit_solution(2698461985018113965)
XLA Ops:
  0.6 3.5 %shard_map.47 = (f32[12,96,128]{2,1,0:T(8,128)}, f32[12,96,128]{2,1,0:T(8,128)}, f32[12,96,128]{2,1,0:T(8,128)}) custom-call(s32[2]{0:T(128)} %pad_add_fusion.refs_0_, f32[6144,128]{1,0:T(8,128)} %bitcast.7), custom_call_target="tpu_custom_call" | custom-call | tf_op jit(solution)/shard_map/pallas_call | solution.py:80
  5.4 3.1 %collective-permute-start = (f32[32,8,8,128]{3,2,1,0:T(8,128)S(1)}, f32[32,8,8,128]{3,2,1,0:T(8,128)S(1)}, u32[]{:S(2)}, u32[]{:S(2)}) collective-permute-start(f32[32,8,8,128]{3,2,1,0:T(8,128)S(1)} %copy-done.3), channel_id=1, source_target_pairs={{0,4},{4,8},{8,12},{12,16},{16,20},{20,24},{24,28},{1,5},{5,9},{9,... | collective-permute-start | bytes 3145736 | tf_op jit(solution)/shard_map/ppermute | solution.py:187
  10.5 5.1 %collective-permute-start.2 = (f32[8,8,128]{2,1,0:T(8,128)S(1)}, f32[8,8,128]{2,1,0:T(8,128)S(1)}, u32[]{:S(2)}, u32[]{:S(2)}) collective-permute-start(f32[8,8,128]{2,1,0:T(8,128)S(1)} %select_multiply_fusion.refs_4_), channel_id=1, source_target_pairs={{0,4},{4,8},{8,12},{12,16},{16,20},{20,24},{24,28},{1,5},{5,9},{9,... | collective-permute-start | bytes 98312 | tf_op jit(solution)/shard_map/ppermute | solution.py:189
  17.7 12.4 %chebyshev.1 = (f32[12,32,128]{2,1,0:T(8,128)}, f32[12,32,128]{2,1,0:T(8,128)}, f32[12,32,128]{2,1,0:T(8,128)}, f32[12,32,128]{2,1,0:T(8,128)}, f32[16,32,128]{2,1,0:T(8,128)}) custom-call(s32[2]{0:T(128)} %pad_add_fusion.refs_0_, f32[2048,128]{1,0:T(8,128)} %bitcast.9, f32[2048,128]{1,0:T(8,128)} %bitcast.11, f32[2048,128]{1,0:T(8,128)} %bitcast.10, ...), custom_call_target="tpu_custom_call" | custom-call | tf_op jit(solution)/shard_map/chebyshev/pallas_call | solution.py:193
  31.8 2.6 %collective-permute-start.5 = (f32[12,32,128]{2,1,0:T(8,128)}, f32[12,32,128]{2,1,0:T(8,128)S(1)}, u32[]{:S(2)}, u32[]{:S(2)}) collective-permute-start(f32[12,32,128]{2,1,0:T(8,128)} %get-tuple-element.55), channel_id=1, source_target_pairs={{0,2},{1,3},{2,0},{3,1},{4,6},{5,7},{6,4},{7,5},{8,10},{9,11},{10,... | collective-permute-start | bytes 589832 | tf_op jit(solution)/shard_map/ppermute | solution.py:21
  35.3 3.5 %collective-permute-start.11 = (f32[12,96,128]{2,1,0:T(8,128)}, f32[12,96,128]{2,1,0:T(8,128)S(1)}, u32[]{:S(2)}, u32[]{:S(2)}) collective-permute-start(f32[12,96,128]{2,1,0:T(8,128)} %get-tuple-element.65), channel_id=1, source_target_pairs={{0,2},{1,3},{2,0},{3,1},{4,6},{5,7},{6,4},{7,5},{8,10},{9,11},{10,... | collective-permute-start | bytes 1769480 | tf_op jit(solution)/shard_map/ppermute | solution.py:21
  38.8 2.0 collective-permute-start.12
  40.8 2.1 collective-permute-done.5.refs_7_
  42.9 3.7 %collective-permute-start.8 = (f32[16,32,128]{2,1,0:T(8,128)}, f32[16,32,128]{2,1,0:T(8,128)S(1)}, u32[]{:S(2)}, u32[]{:S(2)}) collective-permute-start(f32[16,32,128]{2,1,0:T(8,128)} %get-tuple-element.57.refs_2_), channel_id=1, source_target_pairs={{0,2},{1,3},{2,0},{3,1},{4,6},{5,7},{6,4},{7,5},{8,10},{9,11},{10,... | collective-permute-start | bytes 786440 | tf_op jit(solution)/shard_map/ppermute | solution.py:21
  46.6 60.9 %collective-permute-done.8.refs_4_ = f32[16,32,128]{2,1,0:T(8,128)S(1)} collective-permute-done((f32[16,32,128]{2,1,0:T(8,128)}, f32[16,32,128]{2,1,0:T(8,128)S(1)}, u32[]{:S(2)}, u32[]{:S(2)}) %collective-permute-start.8) | collective-permute-done | bytes 262176 | tf_op jit(solution)/shard_map/ppermute | solution.py:21
  107.4 3.9 %shard_map.46 = (f32[12,96,128]{2,1,0:T(8,128)}, f32[16,96,128]{2,1,0:T(8,128)}, f32[4,96,128]{2,1,0:T(8,128)}, f32[4,96,128]{2,1,0:T(8,128)}, f32[4,96,128]{2,1,0:T(8,128)}, /*index=5*/f32[4,96,128]{2,1,0:T(8,128)}) custom-call(s32[2]{0:T(128)} %pad_add_fusion.refs_0_, f32[6144,128]{1,0:T(8,128)} %bitcast.8), custom_call_target="tpu_custom_call" | custom-call | tf_op jit(solution)/shard_map/pallas_call | solution.py:80
  112.6 4.6 %shard_map.48 = (f32[12,128,128]{2,1,0:T(8,128)}, f32[96,128]{1,0:T(8,128)}, f32[96,128]{1,0:T(8,128)}, f32[96,128]{1,0:T(8,128)}, f32[96,128]{1,0:T(8,128)}) custom-call(s32[2]{0:T(128)} %pad_add_fusion.refs_0_, f32[12,96,128]{2,1,0:T(8,128)} %get-tuple-element.63.refs_1_.refs_5_, f32[12,96,128]{2,1,0:T(8,128)} %copy-done, f32[12,96,128]{2,1,0:T(8,128)} %copy-done.1, ...), custom_call_target="tpu_custom_call" | custom-call | tf_op jit(solution)/shard_map/pallas_call | solution.py:33
  117.1 2.0 collective-permute-start.13
  121.6 3.2 %collective-permute-done.14.refs_8_ = f32[96,128]{1,0:T(8,128)S(1)} collective-permute-done((f32[96,128]{1,0:T(8,128)}, f32[96,128]{1,0:T(8,128)S(1)}, u32[]{:S(2)}, u32[]{:S(2)}) %collective-permute-start.14) | collective-permute-done | bytes 49184 | tf_op jit(solution)/shard_map/ppermute | solution.py:21
  127.2 3.3 %shard_map.49 = (f32[16,128,128]{2,1,0:T(8,128)}, f32[96,128]{1,0:T(8,128)}) custom-call(s32[2]{0:T(128)} %pad_add_fusion.refs_0_, f32[16,96,128]{2,1,0:T(8,128)} %get-tuple-element.47.refs_1_, f32[16,32,128]{2,1,0:T(8,128)} %get-tuple-element.57.refs_2_, f32[16,32,128]{2,1,0:T(8,128)} %copy-done.7, f32[16,32,128]{2,1,0:T(8,128)} %copy-done.6, ...), custom_call_target="tpu_custom_call" | custom-call | tf_op jit(solution)/shard_map/pallas_call | solution.py:33
  130.5 5.9 %collective-permute-start.16 = (f32[96,128]{1,0:T(8,128)}, f32[96,128]{1,0:T(8,128)S(1)}, u32[]{:S(2)}, u32[]{:S(2)}) collective-permute-start(f32[96,128]{1,0:T(8,128)} %get-tuple-element.75), channel_id=1, source_target_pairs={{0,4},{4,0},{8,12},{12,8},{16,20},{20,16},{24,28},{28,24},{1,5},{5... | collective-permute-start | bytes 147464 | tf_op jit(solution)/shard_map/ppermute | solution.py:21
  138.4 3.9 %collective-permute-start.19 = (f32[96,128]{1,0:T(8,128)S(1)}, f32[96,128]{1,0:T(8,128)S(1)}, u32[]{:S(2)}, u32[]{:S(2)}) collective-permute-start(f32[96,128]{1,0:T(8,128)S(1)} %add.38), channel_id=1, source_target_pairs={{0,24},{4,28},{8,16},{12,20},{16,8},{20,12},{24,0},{28,4},{1,25},{... | collective-permute-start | bytes 147464 | tf_op jit(solution)/shard_map/ppermute | solution.py:21
  142.2 14.9 %collective-permute-start.18 = (f32[96,128]{1,0:T(8,128)S(1)}, f32[96,128]{1,0:T(8,128)S(1)}, u32[]{:S(2)}, u32[]{:S(2)}) collective-permute-start(f32[96,128]{1,0:T(8,128)S(1)} %add.38), channel_id=1, source_target_pairs={{0,16},{4,20},{8,24},{12,28},{16,0},{20,4},{24,8},{28,12},{1,17},{... | collective-permute-start | bytes 147464 | tf_op jit(solution)/shard_map/ppermute | solution.py:21
  158.6 1.9 collective-permute-start.24
  160.5 2.5 %collective-permute-start.25 = (f32[4,96,128]{2,1,0:T(8,128)S(1)}, f32[4,96,128]{2,1,0:T(8,128)S(1)}, u32[]{:S(2)}, u32[]{:S(2)}) collective-permute-start(f32[4,96,128]{2,1,0:T(8,128)S(1)} %copy-done.32), channel_id=1, source_target_pairs={{0,3},{1,2},{2,1},{3,0},{4,7},{5,6},{6,5},{7,4},{8,11},{9,10},{10,... | collective-permute-start | bytes 589832 | tf_op jit(solution)/shard_map/ppermute | solution.py:21
  164.4 4.2 %collective-permute-done.23.refs_10_ = f32[4,96,128]{2,1,0:T(8,128)S(1)} collective-permute-done((f32[4,96,128]{2,1,0:T(8,128)}, f32[4,96,128]{2,1,0:T(8,128)S(1)}, u32[]{:S(2)}, u32[]{:S(2)}) %collective-permute-start.23) | collective-permute-done | bytes 196640 | tf_op jit(solution)/shard_map/ppermute | solution.py:21
  168.6 9.2 %collective-permute-done.24.refs_11_ = f32[4,96,128]{2,1,0:T(8,128)S(1)} collective-permute-done((f32[4,96,128]{2,1,0:T(8,128)S(1)}, f32[4,96,128]{2,1,0:T(8,128)S(1)}, u32[]{:S(2)}, u32[]{:S(2)}) %collective-permute-start.24) | collective-permute-done | bytes 196640 | tf_op jit(solution)/shard_map/ppermute | solution.py:21
  177.9 4.9 %collective-permute-done.21.refs_3_ = f32[96,128]{1,0:T(8,128)S(1)} collective-permute-done((f32[96,128]{1,0:T(8,128)S(1)}, f32[96,128]{1,0:T(8,128)S(1)}, u32[]{:S(2)}, u32[]{:S(2)}) %collective-permute-start.21) | collective-permute-done | bytes 49184 | tf_op jit(solution)/shard_map/ppermute | solution.py:21
  183.4 6.7 %shard_map.50 = (f32[128,2048]{1,0:T(8,128)}, f32[64,128]{1,0:T(8,128)}, f32[64,128]{1,0:T(8,128)}) custom-call(s32[2]{0:T(128)} %pad_add_fusion.refs_0_, f32[96,128]{1,0:T(8,128)} %copy-done.12, f32[96,128]{1,0:T(8,128)} %copy-done.23, f32[96,128]{1,0:T(8,128)} %copy-done.22, f32[96,128]{1,0:T(8,128)} %copy-done.21, ...), custom_call_target="tpu_custom_call" | custom-call | tf_op jit(solution)/shard_map/pallas_call | solution.py:33
  198.3 1.8 collective-permute-start.32
  200.2 2.6 %collective-permute-start.30 = (f32[64,128]{1,0:T(8,128)S(1)}, f32[64,128]{1,0:T(8,128)S(1)}, u32[]{:S(2)}, u32[]{:S(2)}) collective-permute-start(f32[64,128]{1,0:T(8,128)S(1)} %add_add_fusion.2), channel_id=1, source_target_pairs={{0,1},{1,0},{2,3},{3,2},{4,5},{5,4},{6,7},{7,6},{8,9},{9,8},{10,11... | collective-permute-start | bytes 98312 | tf_op jit(solution)/shard_map/ppermute | solution.py:21
  206.9 7.0 %shard_map.51 = (f32[16,32,128]{2,1,0:T(8,128)}, f32[16,32,128]{2,1,0:T(8,128)}, f32[16,32,128]{2,1,0:T(8,128)}, f32[16,32,128]{2,1,0:T(8,128)}) custom-call(s32[2]{0:T(128)} %pad_add_fusion.refs_0_, f32[64,128]{1,0:T(8,128)} %copy-done.20, f32[64,128]{1,0:T(8,128)} %copy-done.29, f32[128,2048]{1,0:T(8,128)} %get-tuple-element.84.refs_3_), custom_call_target="tpu_custom_call" | custom-call | tf_op jit(solution)/shard_map/pallas_call | solution.py:33
  213.9 1.7 collective-permute-start.34
  216.5 1.8 collective-permute-start.36
  218.3 8.9 %collective-permute-done.34.refs_2_ = f32[16,32,128]{2,1,0:T(8,128)S(1)} collective-permute-done((f32[16,32,128]{2,1,0:T(8,128)}, f32[16,32,128]{2,1,0:T(8,128)S(1)}, u32[]{:S(2)}, u32[]{:S(2)}) %collective-permute-start.34) | collective-permute-done | bytes 262176 | tf_op jit(solution)/shard_map/ppermute | solution.py:21
  227.2 9.9 %collective-permute-done.35.refs_3_ = f32[16,32,128]{2,1,0:T(8,128)S(1)} collective-permute-done((f32[16,32,128]{2,1,0:T(8,128)}, f32[16,32,128]{2,1,0:T(8,128)S(1)}, u32[]{:S(2)}, u32[]{:S(2)}) %collective-permute-start.35) | collective-permute-done | bytes 262176 | tf_op jit(solution)/shard_map/ppermute | solution.py:21
  237.9 3.1 %shard_map.52 = f32[2048,128]{1,0:T(8,128)} custom-call(s32[2]{0:T(128)} %pad_add_fusion.refs_0_, f32[16,32,128]{2,1,0:T(8,128)} %get-tuple-element.85.refs_1_, f32[16,32,128]{2,1,0:T(8,128)} %copy-done.9, f32[16,32,128]{2,1,0:T(8,128)} %copy-done.10, f32[16,32,128]{2,1,0:T(8,128)} %copy-done.11), custom_call_target="tpu_custom_call" | custom-call | tf_op jit(solution)/shard_map/pallas_call | solution.py:33
  (127 shorter events, 34.1 us)
Async XLA Ops:
  4.1 12.3 %collective-permute-start.1 = (f32[32,8,8,128]{3,2,1,0:T(8,128)S(1)}, f32[32,8,8,128]{3,2,1,0:T(8,128)S(1)}, u32[]{:S(2)}, u32[]{:S(2)}) collective-permute-start(f32[32,8,8,128]{3,2,1,0:T(8,128)S(1)} %copy-done.3), channel_id=1, source_target_pairs={{4,0},{8,4},{12,8},{16,12},{20,16},{24,20},{28,24},{5,1},{9,5},{13... | collective-permute-start | bytes 3145736 | tf_op jit(solution)/shard_map/ppermute | solution.py:188
  5.4 11.1 %collective-permute-start = (f32[32,8,8,128]{3,2,1,0:T(8,128)S(1)}, f32[32,8,8,128]{3,2,1,0:T(8,128)S(1)}, u32[]{:S(2)}, u32[]{:S(2)}) collective-permute-start(f32[32,8,8,128]{3,2,1,0:T(8,128)S(1)} %copy-done.3), channel_id=1, source_target_pairs={{0,4},{4,8},{8,12},{12,16},{16,20},{20,24},{24,28},{1,5},{5,9},{9,... | collective-permute-start | bytes 3145736 | tf_op jit(solution)/shard_map/ppermute | solution.py:187
  9.2 6.4 %collective-permute-start.3 = (f32[8,8,128]{2,1,0:T(8,128)S(1)}, f32[8,8,128]{2,1,0:T(8,128)S(1)}, u32[]{:S(2)}, u32[]{:S(2)}) collective-permute-start(f32[8,8,128]{2,1,0:T(8,128)S(1)} %select_multiply_fusion.refs_4_), channel_id=1, source_target_pairs={{4,0},{8,4},{12,8},{16,12},{20,16},{24,20},{28,24},{5,1},{9,5},{13... | collective-permute-start | bytes 98312 | tf_op jit(solution)/shard_map/ppermute | solution.py:190
  10.5 5.9 %collective-permute-start.2 = (f32[8,8,128]{2,1,0:T(8,128)S(1)}, f32[8,8,128]{2,1,0:T(8,128)S(1)}, u32[]{:S(2)}, u32[]{:S(2)}) collective-permute-start(f32[8,8,128]{2,1,0:T(8,128)S(1)} %select_multiply_fusion.refs_4_), channel_id=1, source_target_pairs={{0,4},{4,8},{8,12},{12,16},{16,20},{20,24},{24,28},{1,5},{5,9},{9,... | collective-permute-start | bytes 98312 | tf_op jit(solution)/shard_map/ppermute | solution.py:189
  30.1 8.6 %collective-permute-start.4 = (f32[12,32,128]{2,1,0:T(8,128)}, f32[12,32,128]{2,1,0:T(8,128)S(1)}, u32[]{:S(2)}, u32[]{:S(2)}) collective-permute-start(f32[12,32,128]{2,1,0:T(8,128)} %get-tuple-element.54), channel_id=1, source_target_pairs={{0,1},{1,0},{2,3},{3,2},{4,5},{5,4},{6,7},{7,6},{8,9},{9,8},{10,11... | collective-permute-start | bytes 589832 | tf_op jit(solution)/shard_map/ppermute | solution.py:21
  31.8 11.1 %collective-permute-start.5 = (f32[12,32,128]{2,1,0:T(8,128)}, f32[12,32,128]{2,1,0:T(8,128)S(1)}, u32[]{:S(2)}, u32[]{:S(2)}) collective-permute-start(f32[12,32,128]{2,1,0:T(8,128)} %get-tuple-element.55), channel_id=1, source_target_pairs={{0,2},{1,3},{2,0},{3,1},{4,6},{5,7},{6,4},{7,5},{8,10},{9,11},{10,... | collective-permute-start | bytes 589832 | tf_op jit(solution)/shard_map/ppermute | solution.py:21
  34.4 8.5 %collective-permute-start.6 = (f32[12,32,128]{2,1,0:T(8,128)}, f32[12,32,128]{2,1,0:T(8,128)S(1)}, u32[]{:S(2)}, u32[]{:S(2)}) collective-permute-start(f32[12,32,128]{2,1,0:T(8,128)} %get-tuple-element.56), channel_id=1, source_target_pairs={{0,3},{1,2},{2,1},{3,0},{4,7},{5,6},{6,5},{7,4},{8,11},{9,10},{10,... | collective-permute-start | bytes 589832 | tf_op jit(solution)/shard_map/ppermute | solution.py:21
  34.6 76.7 %collective-permute-start.10 = (f32[12,96,128]{2,1,0:T(8,128)}, f32[12,96,128]{2,1,0:T(8,128)S(1)}, u32[]{:S(2)}, u32[]{:S(2)}) collective-permute-start(f32[12,96,128]{2,1,0:T(8,128)} %get-tuple-element.64), channel_id=1, source_target_pairs={{0,1},{1,0},{2,3},{3,2},{4,5},{5,4},{6,7},{7,6},{8,9},{9,8},{10,11... | collective-permute-start | bytes 1769480 | tf_op jit(solution)/shard_map/ppermute | solution.py:21
  35.3 76.1 %collective-permute-start.11 = (f32[12,96,128]{2,1,0:T(8,128)}, f32[12,96,128]{2,1,0:T(8,128)S(1)}, u32[]{:S(2)}, u32[]{:S(2)}) collective-permute-start(f32[12,96,128]{2,1,0:T(8,128)} %get-tuple-element.65), channel_id=1, source_target_pairs={{0,2},{1,3},{2,0},{3,1},{4,6},{5,7},{6,4},{7,5},{8,10},{9,11},{10,... | collective-permute-start | bytes 1769480 | tf_op jit(solution)/shard_map/ppermute | solution.py:21
  38.8 72.6 %collective-permute-start.12 = (f32[12,96,128]{2,1,0:T(8,128)}, f32[12,96,128]{2,1,0:T(8,128)S(1)}, u32[]{:S(2)}, u32[]{:S(2)}) collective-permute-start(f32[12,96,128]{2,1,0:T(8,128)} %get-tuple-element.66), channel_id=1, source_target_pairs={{0,3},{1,2},{2,1},{3,0},{4,7},{5,6},{6,5},{7,4},{8,11},{9,10},{10,... | collective-permute-start | bytes 1769480 | tf_op jit(solution)/shard_map/ppermute | solution.py:21
  42.9 64.6 %collective-permute-start.8 = (f32[16,32,128]{2,1,0:T(8,128)}, f32[16,32,128]{2,1,0:T(8,128)S(1)}, u32[]{:S(2)}, u32[]{:S(2)}) collective-permute-start(f32[16,32,128]{2,1,0:T(8,128)} %get-tuple-element.57.refs_2_), channel_id=1, source_target_pairs={{0,2},{1,3},{2,0},{3,1},{4,6},{5,7},{6,4},{7,5},{8,10},{9,11},{10,... | collective-permute-start | bytes 786440 | tf_op jit(solution)/shard_map/ppermute | solution.py:21
  46.5 79.9 %collective-permute-start.7 = (f32[16,32,128]{2,1,0:T(8,128)}, f32[16,32,128]{2,1,0:T(8,128)S(1)}, u32[]{:S(2)}, u32[]{:S(2)}) collective-permute-start(f32[16,32,128]{2,1,0:T(8,128)} %get-tuple-element.57.refs_2_), channel_id=1, source_target_pairs={{0,1},{1,0},{2,3},{3,2},{4,5},{5,4},{6,7},{7,6},{8,9},{9,8},{10,11... | collective-permute-start | bytes 786440 | tf_op jit(solution)/shard_map/ppermute | solution.py:21
  107.4 19.0 %collective-permute-start.9 = (f32[16,32,128]{2,1,0:T(8,128)S(1)}, f32[16,32,128]{2,1,0:T(8,128)S(1)}, u32[]{:S(2)}, u32[]{:S(2)}) collective-permute-start(f32[16,32,128]{2,1,0:T(8,128)S(1)} %collective-permute-done.8.refs_4_), channel_id=1, source_target_pairs={{0,1},{1,0},{2,3},{3,2},{4,5},{5,4},{6,7},{7,6},{8,9},{9,8},{10,11... | collective-permute-start | bytes 786440 | tf_op jit(solution)/shard_map/ppermute | solution.py:21
  119.1 5.7 %collective-permute-start.14 = (f32[96,128]{1,0:T(8,128)}, f32[96,128]{1,0:T(8,128)S(1)}, u32[]{:S(2)}, u32[]{:S(2)}) collective-permute-start(f32[96,128]{1,0:T(8,128)} %get-tuple-element.73), channel_id=1, source_target_pairs={{0,2},{1,3},{2,0},{3,1},{4,6},{5,7},{6,4},{7,5},{8,10},{9,11},{10,... | collective-permute-start | bytes 147464 | tf_op jit(solution)/shard_map/ppermute | solution.py:21
  120.2 6.2 %collective-permute-start.15 = (f32[96,128]{1,0:T(8,128)}, f32[96,128]{1,0:T(8,128)S(1)}, u32[]{:S(2)}, u32[]{:S(2)}) collective-permute-start(f32[96,128]{1,0:T(8,128)} %get-tuple-element.74), channel_id=1, source_target_pairs={{0,3},{1,2},{2,1},{3,0},{4,7},{5,6},{6,5},{7,4},{8,11},{9,10},{10,... | collective-permute-start | bytes 147464 | tf_op jit(solution)/shard_map/ppermute | solution.py:21
  130.5 7.0 %collective-permute-start.16 = (f32[96,128]{1,0:T(8,128)}, f32[96,128]{1,0:T(8,128)S(1)}, u32[]{:S(2)}, u32[]{:S(2)}) collective-permute-start(f32[96,128]{1,0:T(8,128)} %get-tuple-element.75), channel_id=1, source_target_pairs={{0,4},{4,0},{8,12},{12,8},{16,20},{20,16},{24,28},{28,24},{1,5},{5... | collective-permute-start | bytes 147464 | tf_op jit(solution)/shard_map/ppermute | solution.py:21
  138.4 22.1 %collective-permute-start.19 = (f32[96,128]{1,0:T(8,128)S(1)}, f32[96,128]{1,0:T(8,128)S(1)}, u32[]{:S(2)}, u32[]{:S(2)}) collective-permute-start(f32[96,128]{1,0:T(8,128)S(1)} %add.38), channel_id=1, source_target_pairs={{0,24},{4,28},{8,16},{12,20},{16,8},{20,12},{24,0},{28,4},{1,25},{... | collective-permute-start | bytes 147464 | tf_op jit(solution)/shard_map/ppermute | solution.py:21
  142.2 20.7 %collective-permute-start.18 = (f32[96,128]{1,0:T(8,128)S(1)}, f32[96,128]{1,0:T(8,128)S(1)}, u32[]{:S(2)}, u32[]{:S(2)}) collective-permute-start(f32[96,128]{1,0:T(8,128)S(1)} %add.38), channel_id=1, source_target_pairs={{0,16},{4,20},{8,24},{12,28},{16,0},{20,4},{24,8},{28,12},{1,17},{... | collective-permute-start | bytes 147464 | tf_op jit(solution)/shard_map/ppermute | solution.py:21
  157.2 5.8 %collective-permute-start.17 = (f32[96,128]{1,0:T(8,128)S(1)}, f32[96,128]{1,0:T(8,128)S(1)}, u32[]{:S(2)}, u32[]{:S(2)}) collective-permute-start(f32[96,128]{1,0:T(8,128)S(1)} %add.38), channel_id=1, source_target_pairs={{0,8},{4,12},{8,0},{12,4},{16,24},{20,28},{24,16},{28,20},{1,9},{5... | collective-permute-start | bytes 147464 | tf_op jit(solution)/shard_map/ppermute | solution.py:21
  158.6 10.1 %collective-permute-start.23 = (f32[4,96,128]{2,1,0:T(8,128)}, f32[4,96,128]{2,1,0:T(8,128)S(1)}, u32[]{:S(2)}, u32[]{:S(2)}) collective-permute-start(f32[4,96,128]{2,1,0:T(8,128)} %get-tuple-element.77), channel_id=1, source_target_pairs={{0,1},{1,0},{2,3},{3,2},{4,5},{5,4},{6,7},{7,6},{8,9},{9,8},{10,11... | collective-permute-start | bytes 589832 | tf_op jit(solution)/shard_map/ppermute | solution.py:21
  158.6 19.3 %collective-permute-start.24 = (f32[4,96,128]{2,1,0:T(8,128)S(1)}, f32[4,96,128]{2,1,0:T(8,128)S(1)}, u32[]{:S(2)}, u32[]{:S(2)}) collective-permute-start(f32[4,96,128]{2,1,0:T(8,128)S(1)} %copy-done.33), channel_id=1, source_target_pairs={{0,2},{1,3},{2,0},{3,1},{4,6},{5,7},{6,4},{7,5},{8,10},{9,11},{10,... | collective-permute-start | bytes 589832 | tf_op jit(solution)/shard_map/ppermute | solution.py:21
  160.5 17.4 %collective-permute-start.25 = (f32[4,96,128]{2,1,0:T(8,128)S(1)}, f32[4,96,128]{2,1,0:T(8,128)S(1)}, u32[]{:S(2)}, u32[]{:S(2)}) collective-permute-start(f32[4,96,128]{2,1,0:T(8,128)S(1)} %copy-done.32), channel_id=1, source_target_pairs={{0,3},{1,2},{2,1},{3,0},{4,7},{5,6},{6,5},{7,4},{8,11},{9,10},{10,... | collective-permute-start | bytes 589832 | tf_op jit(solution)/shard_map/ppermute | solution.py:21
  163.0 14.9 %collective-permute-start.22 = (f32[96,128]{1,0:T(8,128)S(1)}, f32[96,128]{1,0:T(8,128)S(1)}, u32[]{:S(2)}, u32[]{:S(2)}) collective-permute-start(f32[96,128]{1,0:T(8,128)S(1)} %add_add_fusion.refs_1_), channel_id=1, source_target_pairs={{0,3},{1,2},{2,1},{3,0},{4,7},{5,6},{6,5},{7,4},{8,11},{9,10},{10,... | collective-permute-start | bytes 147464 | tf_op jit(solution)/shard_map/ppermute | solution.py:21
  164.4 18.4 %collective-permute-start.21 = (f32[96,128]{1,0:T(8,128)S(1)}, f32[96,128]{1,0:T(8,128)S(1)}, u32[]{:S(2)}, u32[]{:S(2)}) collective-permute-start(f32[96,128]{1,0:T(8,128)S(1)} %add_add_fusion.refs_1_), channel_id=1, source_target_pairs={{0,2},{1,3},{2,0},{3,1},{4,6},{5,7},{6,4},{7,5},{8,10},{9,11},{10,... | collective-permute-start | bytes 147464 | tf_op jit(solution)/shard_map/ppermute | solution.py:21
  168.6 14.2 %collective-permute-start.20 = (f32[96,128]{1,0:T(8,128)S(1)}, f32[96,128]{1,0:T(8,128)S(1)}, u32[]{:S(2)}, u32[]{:S(2)}) collective-permute-start(f32[96,128]{1,0:T(8,128)S(1)} %add_add_fusion.refs_1_), channel_id=1, source_target_pairs={{0,1},{1,0},{2,3},{3,2},{4,5},{5,4},{6,7},{7,6},{8,9},{9,8},{10,11... | collective-permute-start | bytes 147464 | tf_op jit(solution)/shard_map/ppermute | solution.py:21
  192.3 4.8 %collective-permute-start.29 = (f32[64,128]{1,0:T(8,128)S(1)}, f32[64,128]{1,0:T(8,128)S(1)}, u32[]{:S(2)}, u32[]{:S(2)}) collective-permute-start(f32[64,128]{1,0:T(8,128)S(1)} %add.42), channel_id=1, source_target_pairs={{0,24},{4,28},{8,16},{12,20},{16,8},{20,12},{24,0},{28,4},{1,25},{... | collective-permute-start | bytes 98312 | tf_op jit(solution)/shard_map/ppermute | solution.py:21
  198.3 5.8 %collective-permute-start.32 = (f32[64,128]{1,0:T(8,128)S(1)}, f32[64,128]{1,0:T(8,128)S(1)}, u32[]{:S(2)}, u32[]{:S(2)}) collective-permute-start(f32[64,128]{1,0:T(8,128)S(1)} %add_add_fusion.2), channel_id=1, source_target_pairs={{0,3},{1,2},{2,1},{3,0},{4,7},{5,6},{6,5},{7,4},{8,11},{9,10},{10,... | collective-permute-start | bytes 98312 | tf_op jit(solution)/shard_map/ppermute | solution.py:21
  200.2 4.9 %collective-permute-start.31 = (f32[64,128]{1,0:T(8,128)S(1)}, f32[64,128]{1,0:T(8,128)S(1)}, u32[]{:S(2)}, u32[]{:S(2)}) collective-permute-start(f32[64,128]{1,0:T(8,128)S(1)} %add_add_fusion.2), channel_id=1, source_target_pairs={{0,2},{1,3},{2,0},{3,1},{4,6},{5,7},{6,4},{7,5},{8,10},{9,11},{10,... | collective-permute-start | bytes 98312 | tf_op jit(solution)/shard_map/ppermute | solution.py:21
  200.2 4.9 %collective-permute-start.30 = (f32[64,128]{1,0:T(8,128)S(1)}, f32[64,128]{1,0:T(8,128)S(1)}, u32[]{:S(2)}, u32[]{:S(2)}) collective-permute-start(f32[64,128]{1,0:T(8,128)S(1)} %add_add_fusion.2), channel_id=1, source_target_pairs={{0,1},{1,0},{2,3},{3,2},{4,5},{5,4},{6,7},{7,6},{8,9},{9,8},{10,11... | collective-permute-start | bytes 98312 | tf_op jit(solution)/shard_map/ppermute | solution.py:21
  213.9 13.3 %collective-permute-start.34 = (f32[16,32,128]{2,1,0:T(8,128)}, f32[16,32,128]{2,1,0:T(8,128)S(1)}, u32[]{:S(2)}, u32[]{:S(2)}) collective-permute-start(f32[16,32,128]{2,1,0:T(8,128)} %get-tuple-element.86), channel_id=1, source_target_pairs={{0,1},{1,0},{2,3},{3,2},{4,5},{5,4},{6,7},{7,6},{8,9},{9,8},{10,11... | collective-permute-start | bytes 786440 | tf_op jit(solution)/shard_map/ppermute | solution.py:21
  215.6 21.5 %collective-permute-start.35 = (f32[16,32,128]{2,1,0:T(8,128)}, f32[16,32,128]{2,1,0:T(8,128)S(1)}, u32[]{:S(2)}, u32[]{:S(2)}) collective-permute-start(f32[16,32,128]{2,1,0:T(8,128)} %get-tuple-element.87), channel_id=1, source_target_pairs={{0,2},{1,3},{2,0},{3,1},{4,6},{5,7},{6,4},{7,5},{8,10},{9,11},{10,... | collective-permute-start | bytes 786440 | tf_op jit(solution)/shard_map/ppermute | solution.py:21
  216.5 20.6 %collective-permute-start.36 = (f32[16,32,128]{2,1,0:T(8,128)}, f32[16,32,128]{2,1,0:T(8,128)S(1)}, u32[]{:S(2)}, u32[]{:S(2)}) collective-permute-start(f32[16,32,128]{2,1,0:T(8,128)} %get-tuple-element.88), channel_id=1, source_target_pairs={{0,3},{1,2},{2,1},{3,0},{4,7},{5,6},{6,5},{7,4},{8,11},{9,10},{10,... | collective-permute-start | bytes 786440 | tf_op jit(solution)/shard_map/ppermute | solution.py:21
  (39 other events, 438.8 us)

commit v2 on v1

--- a/solution.py
+++ b/solution.py
@@ -45,15 +45,28 @@
     )
 
 
+def halved(x):
+    high = x.astype(jnp.bfloat16)
+    return high, (x - high.astype(F32)).astype(jnp.bfloat16)
+
+
+def dot3(a, b, da, db):
+    (ah, al), (bh, bl) = halved(a), halved(b)
+    one = lambda x, y: lax.dot_general(
+        x, y, (((da,), (db,)), ((), ())), preferred_element_type=F32
+    )
+    return one(ah, bh) + (one(ah, bl) + one(al, bh))
+
+
 def in_line(ref):
     return jnp.concatenate([ref[r] for r in range(ref.shape[0])], axis=1)
 
 
-def near_kernel(place, modes, *outs, total):
+def near_kernel(place, modes, *outs, total, ks):
     count = modes.shape[0] // total
     share = outs[0].shape[0]
-    for k, out in enumerate(outs):
-        start = (place[0] ^ (k + 1)) * share
+    for k, out in zip(ks, outs):
+        start = (place[0] ^ k) * share
         for i in range(share):
             out[i] = modes[pl.ds(start + i, count, stride=total), :]
 
@@ -225,7 +238,7 @@
     gather_fields(place, pieces, fields)
     own = in_line(fields)
     stack = jnp.concatenate([in_line(m) for m in modes], axis=0)
-    value = dot(stack, own, 1, 1)
+    value = dot3(stack, own, 1, 1)
     size = outs[0].shape[0]
     for k, out in enumerate(outs):
         out[...] = value[k * size : (k + 1) * size]
@@ -234,7 +247,7 @@
 def far_correlate_kernel(place, modes, *refs, parts):
     pieces, sums, fields, out = refs[:parts], refs[parts : 2 * parts], refs[2 * parts], refs[2 * parts + 1]
     gather_fields(place, pieces, fields)
-    value = dot(in_line(modes), in_line(fields), 1, 1)
+    value = dot3(in_line(modes), in_line(fields), 1, 1)
     for s in sums:
         value = value + s[...]
     out[...] = value
@@ -264,9 +277,9 @@
         [jnp.concatenate([in_line(a), in_line(b)], axis=1) for a, b in zip(near, far)], axis=0
     )
     stack = jnp.concatenate([c[...] for c in corr], axis=0)
-    value = jnp.concatenate(fields, axis=1) - dot(stack, modes, 0, 0)
+    value = jnp.concatenate(fields, axis=1) - dot3(stack, modes, 0, 0)
     deflated[...] = value
-    halves(place[1], dot(value, value, 1, 1), mine, other)
+    halves(place[1], dot3(value, value, 1, 1), mine, other)
 
 
 def lower_inverse(aug, out, count):
@@ -333,7 +346,7 @@
     order = [
         inverse[pl.ds(pl.multiple_of((place[0] ^ k) * size, TILE), size), :] for k in range(len(outs))
     ]
-    value = dot(scale * jnp.concatenate(order, axis=0), deflated[...], 1, 0)
+    value = dot3(scale * jnp.concatenate(order, axis=0), deflated[...], 1, 0)
     for k, out in enumerate(outs):
         for i in range(rows):
             out[i] = value[k * size : (k + 1) * size, i * nx : (i + 1) * nx]
@@ -406,11 +419,19 @@
 
     modes = locked_modes.reshape(-1, nx)
     block = own_modes // 2 if own_modes % (2 * TILE) == 0 else own_modes
-    near_modes = split_modes(
-        near_kernel, place, modes, [(near_share, own_modes, nx)] * (parts - 1), block
-    )
-    start_block, *near_modes = lax.optimization_barrier([start_block] + list(near_modes))
-    near_modes = exchanged([None] + near_modes)
+    near_modes = [None] * parts
+    for some in (order[:1], order[1:]):
+        got = split_modes(
+            lambda *refs, total: near_kernel(*refs, total=total, ks=some),
+            place,
+            modes,
+            [(near_share, own_modes, nx)] * len(some),
+            block,
+        )
+        for k, x in zip(some, got):
+            near_modes[k] = x
+    start_block, near_modes[order[-1]] = lax.optimization_barrier([start_block, near_modes[order[-1]]])
+    near_modes = exchanged(near_modes)
     near_modes[0], far_own, *far_modes = split_modes(
         far_kernel,
         place,
@@ -427,7 +448,6 @@
         place, start_block, coef_own, clamped, near_rows, far_rows, parts
     )
     near_fields = exchanged(near_fields)
-    far_field, *near_fields = lax.optimization_barrier([far_field] + near_fields)
     far_fields = gathered(far_field)
 
     near_all, *sums = call(
@@ -437,8 +457,8 @@
         [(near_share, count, nx)] + [(own_modes, count)] * parts,
     )
     sums = exchanged(sums)
-    middle = parts // 2
-    *far_modes, far_fields[middle] = lax.optimization_barrier(far_modes + [far_fields[middle]])
+    held = lax.optimization_barrier(far_modes + far_fields)
+    far_modes, far_fields = held[:parts], held[parts:]
     far_modes = exchanged(far_modes)
     far_all, corr = call(
         lambda *refs: far_correlate_kernel(*refs, parts=parts),
@@ -466,12 +486,14 @@
         scratch=[(count, 2 * count), (count, count)],
     )
     outs = exchanged(list(outs))
-    (basis,) = call(
+    basis = pl.pallas_call(
         lambda *refs: place_kernel(*refs, near_share=near_share, far_share=far_share, near_rows=near_rows),
-        place,
-        outs,
-        [(own_count * rows, nx)],
-    )
+        grid=(own_count // TILE,),
+        in_specs=[smem()] + [pl.BlockSpec((near_share + far_share, TILE, nx), lambda g: (0, g, 0))] * parts,
+        out_specs=pl.BlockSpec((TILE * rows, nx), lambda g: (g, 0)),
+        out_shape=jax.ShapeDtypeStruct((own_count * rows, nx), F32),
+        name="place",
+    )(place, *outs)
     return basis.reshape(start_block.shape)
 
 
@@ -484,6 +506,4 @@
     )
     out_specs = P("blk", "slab", None, None)
 
-    return jax.shard_map(
-        per_device, mesh=mesh, in_specs=in_specs, out_specs=out_specs, check_vma=False
-    )
+    return jax.shard_map(per_device, mesh=mesh, in_specs=in_specs, out_specs=out_specs, check_vma=False)

time: 244 us -> 218 us (0.89)
  starting transfers between devices: 73.9 us -> 60 us
  waiting for transfers between devices: 114 us -> 103 us
    ppermute x33, starting transfers between devices: 63.1 us -> 49.1 us  [swap(): lax.ppermute(x, axis, [(i, i ^ bits) for i in range(lax.axis_size(axis))])]
    ppermute x33, waiting for transfers between devices: 113 us -> 103 us  [swap(): lax.ppermute(x, axis, [(i, i ^ bits) for i in range(lax.axis_size(axis))])]
    pallas_call x5 -> x4, Pallas kernels: 24.7 us -> 18.9 us  [call(): pl.pallas_call(kernel, in_specs=[smem()] + [whole(a.shape) for a in args]...]
    pallas_call x0 -> x1, Pallas kernels: none -> 3.61 us  [per_device(): pl.pallas_call(lambda *refs: place_kernel(*refs, near_share=near_share, f...]
    pallas_call x2 -> x3, Pallas kernels: 7.35 us -> 9.69 us  [split_modes(): pl.pallas_call(lambda *refs: kernel(*refs, total=total), grid=(outs[0][1]...]
    unnamed x68 -> x64, local copies, waits for them, and re-layouts: 5.29 us -> 4.08 us
  transfers between devices with their start and end apart: 37 -> 37, of which waited for: 18 -> 19; matrix products, arithmetic and copies ran while one was open for 0% -> 0% of each run, Pallas kernels for 3% -> 10%
where the time goes in v2:
time: 218 us; the launch traced here: 215 us
  waiting for transfers between devices  103 us (47%)
  starting transfers between devices  60 us (28%)
  Pallas kernels  44.6 us (20%)
  local copies, waits for them, and re-layouts  4.08 us (2%)
  other arithmetic  2.89 us (1%)
    ppermute x33, waiting for transfers between devices, swap(): lax.ppermute(x, axis, [(i, i ^ bits) for i in range(lax.axis_size(axis))])  103 us
    ppermute x33, starting transfers between devices, swap(): lax.ppermute(x, axis, [(i, i ^ bits) for i in range(lax.axis_size(axis))])  49.1 us
    pallas_call x4, Pallas kernels, call(): pl.pallas_call(kernel, in_specs=[smem()] + [whole(a.shape) for a in args]...  18.9 us
    pallas_call x1, Pallas kernels, filtered_rows(): pl.pallas_call(lambda *refs: filter_kernel(*refs, steps=DEGREE, ny=ny), g...  12.4 us
    pallas_call x3, Pallas kernels, split_modes(): pl.pallas_call(lambda *refs: kernel(*refs, total=total), grid=(outs[0][1]...  9.69 us
  transfers between devices with their start and end apart: 37, of which 19 were waited for; matrix products, arithmetic and copies ran while one was open for 0% of the time, Pallas kernels for 10%

profile of v2, /device:TPU:0, one launch (start us, length us, event | category | flops | bytes accessed | tf_op | source)
XLA Modules:
  0.0 215.1 jit_solution(7174783533645154667)
XLA Ops:
  0.6 3.1 %shard_map.47 = (f32[12,96,128]{2,1,0:T(8,128)}, f32[12,96,128]{2,1,0:T(8,128)}) custom-call(s32[2]{0:T(128)} %pad_add_fusion.refs_0_, f32[6144,128]{1,0:T(8,128)} %bitcast.7), custom_call_target="tpu_custom_call" | custom-call | tf_op jit(solution)/shard_map/pallas_call | solution.py:93
  5.1 4.1 %collective-permute-start = (f32[32,8,8,128]{3,2,1,0:T(8,128)S(1)}, f32[32,8,8,128]{3,2,1,0:T(8,128)}, u32[]{:S(2)}, u32[]{:S(2)}) collective-permute-start(f32[32,8,8,128]{3,2,1,0:T(8,128)S(1)} %copy-done.3), channel_id=1, source_target_pairs={{0,4},{4,8},{8,12},{12,16},{16,20},{20,24},{24,28},{1,5},{5,9},{9,... | collective-permute-start | bytes 3145736 | tf_op jit(solution)/shard_map/ppermute | solution.py:200
  11.2 4.1 %collective-permute-start.2 = (f32[8,8,128]{2,1,0:T(8,128)S(1)}, f32[8,8,128]{2,1,0:T(8,128)S(1)}, u32[]{:S(2)}, u32[]{:S(2)}) collective-permute-start(f32[8,8,128]{2,1,0:T(8,128)S(1)} %select_multiply_fusion.refs_4_), channel_id=1, source_target_pairs={{0,4},{4,8},{8,12},{12,16},{16,20},{20,24},{24,28},{1,5},{5,9},{9,... | collective-permute-start | bytes 98312 | tf_op jit(solution)/shard_map/ppermute | solution.py:202
  15.4 2.8 %shard_map.48 = f32[12,96,128]{2,1,0:T(8,128)} custom-call(s32[2]{0:T(128)} %pad_add_fusion.refs_0_, f32[6144,128]{1,0:T(8,128)} %bitcast.8), custom_call_target="tpu_custom_call" | custom-call | tf_op jit(solution)/shard_map/pallas_call | solution.py:93
  18.2 3.0 %collective-permute-start.8 = (f32[12,96,128]{2,1,0:T(8,128)}, f32[12,96,128]{2,1,0:T(8,128)S(1)}, u32[]{:S(2)}, u32[]{:S(2)}) collective-permute-start(f32[12,96,128]{2,1,0:T(8,128)} %shard_map.48), channel_id=1, source_target_pairs={{0,2},{1,3},{2,0},{3,1},{4,6},{5,7},{6,4},{7,5},{8,10},{9,11},{10,... | collective-permute-start | bytes 1769480 | tf_op jit(solution)/shard_map/ppermute | solution.py:21
  23.4 12.4 %chebyshev.1 = (f32[12,32,128]{2,1,0:T(8,128)}, f32[12,32,128]{2,1,0:T(8,128)}, f32[12,32,128]{2,1,0:T(8,128)}, f32[12,32,128]{2,1,0:T(8,128)}, f32[16,32,128]{2,1,0:T(8,128)}) custom-call(s32[2]{0:T(128)} %pad_add_fusion.refs_0_, f32[2048,128]{1,0:T(8,128)} %bitcast.10, f32[2048,128]{1,0:T(8,128)} %bitcast.4.refs_2_, f32[2048,128]{1,0:T(8,128)} %bitcast.5.refs_3_, ...), custom_call_target="tpu_custom_call" | custom-call | tf_op jit(solution)/shard_map/chebyshev/pallas_call | solution.py:206
  37.2 2.5 %collective-permute-start.4 = (f32[16,32,128]{2,1,0:T(8,128)}, f32[16,32,128]{2,1,0:T(8,128)S(1)}, u32[]{:S(2)}, u32[]{:S(2)}) collective-permute-start(f32[16,32,128]{2,1,0:T(8,128)} %get-tuple-element.50.refs_2_), channel_id=1, source_target_pairs={{0,1},{1,0},{2,3},{3,2},{4,5},{5,4},{6,7},{7,6},{8,9},{9,8},{10,11... | collective-permute-start | bytes 786440 | tf_op jit(solution)/shard_map/ppermute | solution.py:21
  39.7 44.3 %collective-permute-done.5.refs_4_ = f32[16,32,128]{2,1,0:T(8,128)S(1)} collective-permute-done((f32[16,32,128]{2,1,0:T(8,128)}, f32[16,32,128]{2,1,0:T(8,128)S(1)}, u32[]{:S(2)}, u32[]{:S(2)}) %collective-permute-start.5) | collective-permute-done | bytes 262176 | tf_op jit(solution)/shard_map/ppermute | solution.py:21
  84.0 1.8 collective-permute-start.6
  86.0 3.1 %collective-permute-start.11 = (f32[12,32,128]{2,1,0:T(8,128)}, f32[12,32,128]{2,1,0:T(8,128)S(1)}, u32[]{:S(2)}, u32[]{:S(2)}) collective-permute-start(f32[12,32,128]{2,1,0:T(8,128)} %get-tuple-element.59), channel_id=1, source_target_pairs={{0,2},{1,3},{2,0},{3,1},{4,6},{5,7},{6,4},{7,5},{8,10},{9,11},{10,... | collective-permute-start | bytes 589832 | tf_op jit(solution)/shard_map/ppermute | solution.py:21
  90.7 3.8 %shard_map.46 = (f32[12,96,128]{2,1,0:T(8,128)}, f32[16,96,128]{2,1,0:T(8,128)}, f32[4,96,128]{2,1,0:T(8,128)}, f32[4,96,128]{2,1,0:T(8,128)}, f32[4,96,128]{2,1,0:T(8,128)}, /*index=5*/f32[4,96,128]{2,1,0:T(8,128)}) custom-call(s32[2]{0:T(128)} %pad_add_fusion.refs_0_, f32[6144,128]{1,0:T(8,128)} %bitcast.9), custom_call_target="tpu_custom_call" | custom-call | tf_op jit(solution)/shard_map/pallas_call | solution.py:93
  94.4 6.8 %collective-permute-done.10.refs_6_ = f32[12,32,128]{2,1,0:T(8,128)S(1)} collective-permute-done((f32[12,32,128]{2,1,0:T(8,128)}, f32[12,32,128]{2,1,0:T(8,128)S(1)}, u32[]{:S(2)}, u32[]{:S(2)}) %collective-permute-start.10) | collective-permute-done | bytes 196640 | tf_op jit(solution)/shard_map/ppermute | solution.py:21
  101.2 6.5 %collective-permute-done.12.refs_8_ = f32[12,32,128]{2,1,0:T(8,128)S(1)} collective-permute-done((f32[12,32,128]{2,1,0:T(8,128)}, f32[12,32,128]{2,1,0:T(8,128)S(1)}, u32[]{:S(2)}, u32[]{:S(2)}) %collective-permute-start.12) | collective-permute-done | bytes 196640 | tf_op jit(solution)/shard_map/ppermute | solution.py:21
  108.4 3.6 %shard_map.49 = (f32[12,128,128]{2,1,0:T(8,128)}, f32[96,128]{1,0:T(8,128)}, f32[96,128]{1,0:T(8,128)}, f32[96,128]{1,0:T(8,128)}, f32[96,128]{1,0:T(8,128)}) custom-call(s32[2]{0:T(128)} %pad_add_fusion.refs_0_, f32[12,96,128]{2,1,0:T(8,128)} %get-tuple-element.54.refs_1_.refs_5_, f32[12,96,128]{2,1,0:T(8,128)} %copy-done.1, f32[12,96,128]{2,1,0:T(8,128)} %copy-done, ...), custom_call_target="tpu_custom_call" | custom-call | tf_op jit(solution)/shard_map/pallas_call | solution.py:33
  112.3 2.2 %collective-permute-start.14 = (f32[96,128]{1,0:T(8,128)}, f32[96,128]{1,0:T(8,128)S(1)}, u32[]{:S(2)}, u32[]{:S(2)}) collective-permute-start(f32[96,128]{1,0:T(8,128)} %get-tuple-element.63), channel_id=1, source_target_pairs={{0,2},{1,3},{2,0},{3,1},{4,6},{5,7},{6,4},{7,5},{8,10},{9,11},{10,... | collective-permute-start | bytes 147464 | tf_op jit(solution)/shard_map/ppermute | solution.py:21
  114.5 2.0 collective-permute-start.15
  116.5 2.6 %collective-permute-done.14.refs_8_ = f32[96,128]{1,0:T(8,128)S(1)} collective-permute-done((f32[96,128]{1,0:T(8,128)}, f32[96,128]{1,0:T(8,128)S(1)}, u32[]{:S(2)}, u32[]{:S(2)}) %collective-permute-start.14) | collective-permute-done | bytes 49184 | tf_op jit(solution)/shard_map/ppermute | solution.py:21
  121.2 2.8 %shard_map.50 = (f32[16,128,128]{2,1,0:T(8,128)}, f32[96,128]{1,0:T(8,128)}) custom-call(s32[2]{0:T(128)} %pad_add_fusion.refs_0_, f32[16,96,128]{2,1,0:T(8,128)} %get-tuple-element.42.refs_1_, f32[16,32,128]{2,1,0:T(8,128)} %get-tuple-element.50.refs_2_, f32[16,32,128]{2,1,0:T(8,128)} %copy-done.5, f32[16,32,128]{2,1,0:T(8,128)} %copy-done.4, ...), custom_call_target="tpu_custom_call" | custom-call | tf_op jit(solution)/shard_map/pallas_call | solution.py:33
  127.1 2.6 %collective-permute-start.18 = (f32[96,128]{1,0:T(8,128)S(1)}, f32[96,128]{1,0:T(8,128)S(1)}, u32[]{:S(2)}, u32[]{:S(2)}) collective-permute-start(f32[96,128]{1,0:T(8,128)S(1)} %add.38), channel_id=1, source_target_pairs={{0,16},{4,20},{8,24},{12,28},{16,0},{20,4},{24,8},{28,12},{1,17},{... | collective-permute-start | bytes 147464 | tf_op jit(solution)/shard_map/ppermute | solution.py:21
  129.8 2.6 %collective-permute-start.24 = (f32[4,96,128]{2,1,0:T(8,128)}, f32[4,96,128]{2,1,0:T(8,128)S(1)}, u32[]{:S(2)}, u32[]{:S(2)}) collective-permute-start(f32[4,96,128]{2,1,0:T(8,128)} %get-tuple-element.68), channel_id=1, source_target_pairs={{0,2},{1,3},{2,0},{3,1},{4,6},{5,7},{6,4},{7,5},{8,10},{9,11},{10,... | collective-permute-start | bytes 589832 | tf_op jit(solution)/shard_map/ppermute | solution.py:21
  132.4 1.8 collective-permute-start.25
  134.2 2.1 collective-permute-start.22
  136.3 10.7 %collective-permute-done.22.refs_4_ = f32[96,128]{1,0:T(8,128)S(1)} collective-permute-done((f32[96,128]{1,0:T(8,128)S(1)}, f32[96,128]{1,0:T(8,128)S(1)}, u32[]{:S(2)}, u32[]{:S(2)}) %collective-permute-start.22) | collective-permute-done | bytes 49184 | tf_op jit(solution)/shard_map/ppermute | solution.py:21
  147.0 7.1 %collective-permute-start.20 = (f32[96,128]{1,0:T(8,128)S(1)}, f32[96,128]{1,0:T(8,128)S(1)}, u32[]{:S(2)}, u32[]{:S(2)}) collective-permute-start(f32[96,128]{1,0:T(8,128)S(1)} %add_add_fusion.refs_1_), channel_id=1, source_target_pairs={{0,1},{1,0},{2,3},{3,2},{4,5},{5,4},{6,7},{7,6},{8,9},{9,8},{10,11... | collective-permute-start | bytes 147464 | tf_op jit(solution)/shard_map/ppermute | solution.py:21
  154.2 2.0 collective-permute-done.20.refs_2_
  157.1 5.6 %shard_map.51 = (f32[128,2048]{1,0:T(8,128)}, f32[64,128]{1,0:T(8,128)}, f32[64,128]{1,0:T(8,128)}) custom-call(s32[2]{0:T(128)} %pad_add_fusion.refs_0_, f32[96,128]{1,0:T(8,128)} %copy-done.10, f32[96,128]{1,0:T(8,128)} %copy-done.21, f32[96,128]{1,0:T(8,128)} %copy-done.20, f32[96,128]{1,0:T(8,128)} %copy-done.19, ...), custom_call_target="tpu_custom_call" | custom-call | tf_op jit(solution)/shard_map/pallas_call | solution.py:33
  172.0 2.4 %collective-permute-start.32 = (f32[64,128]{1,0:T(8,128)S(1)}, f32[64,128]{1,0:T(8,128)S(1)}, u32[]{:S(2)}, u32[]{:S(2)}) collective-permute-start(f32[64,128]{1,0:T(8,128)S(1)} %add_add_fusion.2), channel_id=1, source_target_pairs={{0,3},{1,2},{2,1},{3,0},{4,7},{5,6},{6,5},{7,4},{8,11},{9,10},{10,... | collective-permute-start | bytes 98312 | tf_op jit(solution)/shard_map/ppermute | solution.py:21
  181.5 6.9 %shard_map.52 = (f32[16,32,128]{2,1,0:T(8,128)}, f32[16,32,128]{2,1,0:T(8,128)}, f32[16,32,128]{2,1,0:T(8,128)}, f32[16,32,128]{2,1,0:T(8,128)}) custom-call(s32[2]{0:T(128)} %pad_add_fusion.refs_0_, f32[64,128]{1,0:T(8,128)} %copy-done.18, f32[64,128]{1,0:T(8,128)} %copy-done.27, f32[128,2048]{1,0:T(8,128)} %get-tuple-element.74.refs_3_), custom_call_target="tpu_custom_call" | custom-call | tf_op jit(solution)/shard_map/pallas_call | solution.py:33
  189.2 2.0 collective-permute-start.35
  192.8 9.2 %collective-permute-done.34.refs_2_ = f32[16,32,128]{2,1,0:T(8,128)S(1)} collective-permute-done((f32[16,32,128]{2,1,0:T(8,128)}, f32[16,32,128]{2,1,0:T(8,128)S(1)}, u32[]{:S(2)}, u32[]{:S(2)}) %collective-permute-start.34) | collective-permute-done | bytes 262176 | tf_op jit(solution)/shard_map/ppermute | solution.py:21
  202.0 8.8 %collective-permute-done.35.refs_3_ = f32[16,32,128]{2,1,0:T(8,128)S(1)} collective-permute-done((f32[16,32,128]{2,1,0:T(8,128)}, f32[16,32,128]{2,1,0:T(8,128)S(1)}, u32[]{:S(2)}, u32[]{:S(2)}) %collective-permute-start.35) | collective-permute-done | bytes 262176 | tf_op jit(solution)/shard_map/ppermute | solution.py:21
  211.5 3.6 %place.1 = f32[2048,128]{1,0:T(8,128)} custom-call(s32[2]{0:T(128)} %pad_add_fusion.refs_0_, f32[16,32,128]{2,1,0:T(8,128)} %get-tuple-element.75.refs_1_, f32[16,32,128]{2,1,0:T(8,128)} %copy-done.7, f32[16,32,128]{2,1,0:T(8,128)} %copy-done.8, f32[16,32,128]{2,1,0:T(8,128)} %copy-done.9), custom_call_target="tpu_custom_call" | custom-call | tf_op jit(solution)/shard_map/place/pallas_call | solution.py:489
  (124 shorter events, 35.9 us)
Async XLA Ops:
  3.7 19.1 %collective-permute-start.1 = (f32[32,8,8,128]{3,2,1,0:T(8,128)S(1)}, f32[32,8,8,128]{3,2,1,0:T(8,128)}, u32[]{:S(2)}, u32[]{:S(2)}) collective-permute-start(f32[32,8,8,128]{3,2,1,0:T(8,128)S(1)} %copy-done.3), channel_id=1, source_target_pairs={{4,0},{8,4},{12,8},{16,12},{20,16},{24,20},{28,24},{5,1},{9,5},{13... | collective-permute-start | bytes 3145736 | tf_op jit(solution)/shard_map/ppermute | solution.py:201
  5.1 17.7 %collective-permute-start = (f32[32,8,8,128]{3,2,1,0:T(8,128)S(1)}, f32[32,8,8,128]{3,2,1,0:T(8,128)}, u32[]{:S(2)}, u32[]{:S(2)}) collective-permute-start(f32[32,8,8,128]{3,2,1,0:T(8,128)S(1)} %copy-done.3), channel_id=1, source_target_pairs={{0,4},{4,8},{8,12},{12,16},{16,20},{20,24},{24,28},{1,5},{5,9},{9,... | collective-permute-start | bytes 3145736 | tf_op jit(solution)/shard_map/ppermute | solution.py:200
  9.9 11.3 %collective-permute-start.3 = (f32[8,8,128]{2,1,0:T(8,128)S(1)}, f32[8,8,128]{2,1,0:T(8,128)S(1)}, u32[]{:S(2)}, u32[]{:S(2)}) collective-permute-start(f32[8,8,128]{2,1,0:T(8,128)S(1)} %select_multiply_fusion.refs_4_), channel_id=1, source_target_pairs={{4,0},{8,4},{12,8},{16,12},{20,16},{24,20},{28,24},{5,1},{9,5},{13... | collective-permute-start | bytes 98312 | tf_op jit(solution)/shard_map/ppermute | solution.py:203
  11.2 11.6 %collective-permute-start.2 = (f32[8,8,128]{2,1,0:T(8,128)S(1)}, f32[8,8,128]{2,1,0:T(8,128)S(1)}, u32[]{:S(2)}, u32[]{:S(2)}) collective-permute-start(f32[8,8,128]{2,1,0:T(8,128)S(1)} %select_multiply_fusion.refs_4_), channel_id=1, source_target_pairs={{0,4},{4,8},{8,12},{12,16},{16,20},{20,24},{24,28},{1,5},{5,9},{9,... | collective-permute-start | bytes 98312 | tf_op jit(solution)/shard_map/ppermute | solution.py:202
  18.2 67.6 %collective-permute-start.8 = (f32[12,96,128]{2,1,0:T(8,128)}, f32[12,96,128]{2,1,0:T(8,128)S(1)}, u32[]{:S(2)}, u32[]{:S(2)}) collective-permute-start(f32[12,96,128]{2,1,0:T(8,128)} %shard_map.48), channel_id=1, source_target_pairs={{0,2},{1,3},{2,0},{3,1},{4,6},{5,7},{6,4},{7,5},{8,10},{9,11},{10,... | collective-permute-start | bytes 1769480 | tf_op jit(solution)/shard_map/ppermute | solution.py:21
  21.2 64.9 %collective-permute-start.7 = (f32[12,96,128]{2,1,0:T(8,128)S(1)}, f32[12,96,128]{2,1,0:T(8,128)S(1)}, u32[]{:S(2)}, u32[]{:S(2)}) collective-permute-start(f32[12,96,128]{2,1,0:T(8,128)S(1)} %copy-done.30), channel_id=1, source_target_pairs={{0,1},{1,0},{2,3},{3,2},{4,5},{5,4},{6,7},{7,6},{8,9},{9,8},{10,11... | collective-permute-start | bytes 1769480 | tf_op jit(solution)/shard_map/ppermute | solution.py:21
  22.8 66.4 %collective-permute-start.9 = (f32[12,96,128]{2,1,0:T(8,128)}, f32[12,96,128]{2,1,0:T(8,128)S(1)}, u32[]{:S(2)}, u32[]{:S(2)}) collective-permute-start(f32[12,96,128]{2,1,0:T(8,128)} %get-tuple-element.56), channel_id=1, source_target_pairs={{0,3},{1,2},{2,1},{3,0},{4,7},{5,6},{6,5},{7,4},{8,11},{9,10},{10,... | collective-permute-start | bytes 1769480 | tf_op jit(solution)/shard_map/ppermute | solution.py:21
  35.8 48.2 %collective-permute-start.5 = (f32[16,32,128]{2,1,0:T(8,128)}, f32[16,32,128]{2,1,0:T(8,128)S(1)}, u32[]{:S(2)}, u32[]{:S(2)}) collective-permute-start(f32[16,32,128]{2,1,0:T(8,128)} %get-tuple-element.50.refs_2_), channel_id=1, source_target_pairs={{0,2},{1,3},{2,0},{3,1},{4,6},{5,7},{6,4},{7,5},{8,10},{9,11},{10,... | collective-permute-start | bytes 786440 | tf_op jit(solution)/shard_map/ppermute | solution.py:21
  37.2 79.2 %collective-permute-start.4 = (f32[16,32,128]{2,1,0:T(8,128)}, f32[16,32,128]{2,1,0:T(8,128)S(1)}, u32[]{:S(2)}, u32[]{:S(2)}) collective-permute-start(f32[16,32,128]{2,1,0:T(8,128)} %get-tuple-element.50.refs_2_), channel_id=1, source_target_pairs={{0,1},{1,0},{2,3},{3,2},{4,5},{5,4},{6,7},{7,6},{8,9},{9,8},{10,11... | collective-permute-start | bytes 786440 | tf_op jit(solution)/shard_map/ppermute | solution.py:21
  84.0 32.5 %collective-permute-start.6 = (f32[16,32,128]{2,1,0:T(8,128)S(1)}, f32[16,32,128]{2,1,0:T(8,128)S(1)}, u32[]{:S(2)}, u32[]{:S(2)}) collective-permute-start(f32[16,32,128]{2,1,0:T(8,128)S(1)} %collective-permute-done.5.refs_4_), channel_id=1, source_target_pairs={{0,1},{1,0},{2,3},{3,2},{4,5},{5,4},{6,7},{7,6},{8,9},{9,8},{10,11... | collective-permute-start | bytes 786440 | tf_op jit(solution)/shard_map/ppermute | solution.py:21
  85.8 15.4 %collective-permute-start.10 = (f32[12,32,128]{2,1,0:T(8,128)}, f32[12,32,128]{2,1,0:T(8,128)S(1)}, u32[]{:S(2)}, u32[]{:S(2)}) collective-permute-start(f32[12,32,128]{2,1,0:T(8,128)} %get-tuple-element.58), channel_id=1, source_target_pairs={{0,1},{1,0},{2,3},{3,2},{4,5},{5,4},{6,7},{7,6},{8,9},{9,8},{10,11... | collective-permute-start | bytes 589832 | tf_op jit(solution)/shard_map/ppermute | solution.py:21
  86.0 15.2 %collective-permute-start.11 = (f32[12,32,128]{2,1,0:T(8,128)}, f32[12,32,128]{2,1,0:T(8,128)S(1)}, u32[]{:S(2)}, u32[]{:S(2)}) collective-permute-start(f32[12,32,128]{2,1,0:T(8,128)} %get-tuple-element.59), channel_id=1, source_target_pairs={{0,2},{1,3},{2,0},{3,1},{4,6},{5,7},{6,4},{7,5},{8,10},{9,11},{10,... | collective-permute-start | bytes 589832 | tf_op jit(solution)/shard_map/ppermute | solution.py:21
  89.2 18.6 %collective-permute-start.12 = (f32[12,32,128]{2,1,0:T(8,128)}, f32[12,32,128]{2,1,0:T(8,128)S(1)}, u32[]{:S(2)}, u32[]{:S(2)}) collective-permute-start(f32[12,32,128]{2,1,0:T(8,128)} %get-tuple-element.60), channel_id=1, source_target_pairs={{0,3},{1,2},{2,1},{3,0},{4,7},{5,6},{6,5},{7,4},{8,11},{9,10},{10,... | collective-permute-start | bytes 589832 | tf_op jit(solution)/shard_map/ppermute | solution.py:21
  112.0 4.4 %collective-permute-start.13 = (f32[96,128]{1,0:T(8,128)}, f32[96,128]{1,0:T(8,128)S(1)}, u32[]{:S(2)}, u32[]{:S(2)}) collective-permute-start(f32[96,128]{1,0:T(8,128)} %get-tuple-element.62), channel_id=1, source_target_pairs={{0,1},{1,0},{2,3},{3,2},{4,5},{5,4},{6,7},{7,6},{8,9},{9,8},{10,11... | collective-permute-start | bytes 147464 | tf_op jit(solution)/shard_map/ppermute | solution.py:21
  112.3 6.8 %collective-permute-start.14 = (f32[96,128]{1,0:T(8,128)}, f32[96,128]{1,0:T(8,128)S(1)}, u32[]{:S(2)}, u32[]{:S(2)}) collective-permute-start(f32[96,128]{1,0:T(8,128)} %get-tuple-element.63), channel_id=1, source_target_pairs={{0,2},{1,3},{2,0},{3,1},{4,6},{5,7},{6,4},{7,5},{8,10},{9,11},{10,... | collective-permute-start | bytes 147464 | tf_op jit(solution)/shard_map/ppermute | solution.py:21
  114.5 6.1 %collective-permute-start.15 = (f32[96,128]{1,0:T(8,128)}, f32[96,128]{1,0:T(8,128)S(1)}, u32[]{:S(2)}, u32[]{:S(2)}) collective-permute-start(f32[96,128]{1,0:T(8,128)} %get-tuple-element.64), channel_id=1, source_target_pairs={{0,3},{1,2},{2,1},{3,0},{4,7},{5,6},{6,5},{7,4},{8,11},{9,10},{10,... | collective-permute-start | bytes 147464 | tf_op jit(solution)/shard_map/ppermute | solution.py:21
  126.3 6.1 %collective-permute-start.19 = (f32[96,128]{1,0:T(8,128)S(1)}, f32[96,128]{1,0:T(8,128)S(1)}, u32[]{:S(2)}, u32[]{:S(2)}) collective-permute-start(f32[96,128]{1,0:T(8,128)S(1)} %add.38), channel_id=1, source_target_pairs={{0,24},{4,28},{8,16},{12,20},{16,8},{20,12},{24,0},{28,4},{1,25},{... | collective-permute-start | bytes 147464 | tf_op jit(solution)/shard_map/ppermute | solution.py:21
  127.1 7.1 %collective-permute-start.18 = (f32[96,128]{1,0:T(8,128)S(1)}, f32[96,128]{1,0:T(8,128)S(1)}, u32[]{:S(2)}, u32[]{:S(2)}) collective-permute-start(f32[96,128]{1,0:T(8,128)S(1)} %add.38), channel_id=1, source_target_pairs={{0,16},{4,20},{8,24},{12,28},{16,0},{20,4},{24,8},{28,12},{1,17},{... | collective-permute-start | bytes 147464 | tf_op jit(solution)/shard_map/ppermute | solution.py:21
  129.7 4.5 %collective-permute-start.17 = (f32[96,128]{1,0:T(8,128)S(1)}, f32[96,128]{1,0:T(8,128)S(1)}, u32[]{:S(2)}, u32[]{:S(2)}) collective-permute-start(f32[96,128]{1,0:T(8,128)S(1)} %add.38), channel_id=1, source_target_pairs={{0,8},{4,12},{8,0},{12,4},{16,24},{20,28},{24,16},{28,20},{1,9},{5... | collective-permute-start | bytes 147464 | tf_op jit(solution)/shard_map/ppermute | solution.py:21
  129.8 26.4 %collective-permute-start.23 = (f32[4,96,128]{2,1,0:T(8,128)}, f32[4,96,128]{2,1,0:T(8,128)S(1)}, u32[]{:S(2)}, u32[]{:S(2)}) collective-permute-start(f32[4,96,128]{2,1,0:T(8,128)} %get-tuple-element.67), channel_id=1, source_target_pairs={{0,1},{1,0},{2,3},{3,2},{4,5},{5,4},{6,7},{7,6},{8,9},{9,8},{10,11... | collective-permute-start | bytes 589832 | tf_op jit(solution)/shard_map/ppermute | solution.py:21
  129.8 26.4 %collective-permute-start.24 = (f32[4,96,128]{2,1,0:T(8,128)}, f32[4,96,128]{2,1,0:T(8,128)S(1)}, u32[]{:S(2)}, u32[]{:S(2)}) collective-permute-start(f32[4,96,128]{2,1,0:T(8,128)} %get-tuple-element.68), channel_id=1, source_target_pairs={{0,2},{1,3},{2,0},{3,1},{4,6},{5,7},{6,4},{7,5},{8,10},{9,11},{10,... | collective-permute-start | bytes 589832 | tf_op jit(solution)/shard_map/ppermute | solution.py:21
  132.4 23.8 %collective-permute-start.25 = (f32[4,96,128]{2,1,0:T(8,128)S(1)}, f32[4,96,128]{2,1,0:T(8,128)S(1)}, u32[]{:S(2)}, u32[]{:S(2)}) collective-permute-start(f32[4,96,128]{2,1,0:T(8,128)S(1)} %copy-done.31), channel_id=1, source_target_pairs={{0,3},{1,2},{2,1},{3,0},{4,7},{5,6},{6,5},{7,4},{8,11},{9,10},{10,... | collective-permute-start | bytes 589832 | tf_op jit(solution)/shard_map/ppermute | solution.py:21
  134.2 12.8 %collective-permute-start.22 = (f32[96,128]{1,0:T(8,128)S(1)}, f32[96,128]{1,0:T(8,128)S(1)}, u32[]{:S(2)}, u32[]{:S(2)}) collective-permute-start(f32[96,128]{1,0:T(8,128)S(1)} %add_add_fusion.refs_1_), channel_id=1, source_target_pairs={{0,3},{1,2},{2,1},{3,0},{4,7},{5,6},{6,5},{7,4},{8,11},{9,10},{10,... | collective-permute-start | bytes 147464 | tf_op jit(solution)/shard_map/ppermute | solution.py:21
  136.3 17.9 %collective-permute-start.21 = (f32[96,128]{1,0:T(8,128)S(1)}, f32[96,128]{1,0:T(8,128)S(1)}, u32[]{:S(2)}, u32[]{:S(2)}) collective-permute-start(f32[96,128]{1,0:T(8,128)S(1)} %add_add_fusion.refs_1_), channel_id=1, source_target_pairs={{0,2},{1,3},{2,0},{3,1},{4,6},{5,7},{6,4},{7,5},{8,10},{9,11},{10,... | collective-permute-start | bytes 147464 | tf_op jit(solution)/shard_map/ppermute | solution.py:21
  147.0 9.2 %collective-permute-start.20 = (f32[96,128]{1,0:T(8,128)S(1)}, f32[96,128]{1,0:T(8,128)S(1)}, u32[]{:S(2)}, u32[]{:S(2)}) collective-permute-start(f32[96,128]{1,0:T(8,128)S(1)} %add_add_fusion.refs_1_), channel_id=1, source_target_pairs={{0,1},{1,0},{2,3},{3,2},{4,5},{5,4},{6,7},{7,6},{8,9},{9,8},{10,11... | collective-permute-start | bytes 147464 | tf_op jit(solution)/shard_map/ppermute | solution.py:21
  164.8 4.8 %collective-permute-start.29 = (f32[64,128]{1,0:T(8,128)S(1)}, f32[64,128]{1,0:T(8,128)S(1)}, u32[]{:S(2)}, u32[]{:S(2)}) collective-permute-start(f32[64,128]{1,0:T(8,128)S(1)} %add.42), channel_id=1, source_target_pairs={{0,24},{4,28},{8,16},{12,20},{16,8},{20,12},{24,0},{28,4},{1,25},{... | collective-permute-start | bytes 98312 | tf_op jit(solution)/shard_map/ppermute | solution.py:21
  172.0 6.0 %collective-permute-start.32 = (f32[64,128]{1,0:T(8,128)S(1)}, f32[64,128]{1,0:T(8,128)S(1)}, u32[]{:S(2)}, u32[]{:S(2)}) collective-permute-start(f32[64,128]{1,0:T(8,128)S(1)} %add_add_fusion.2), channel_id=1, source_target_pairs={{0,3},{1,2},{2,1},{3,0},{4,7},{5,6},{6,5},{7,4},{8,11},{9,10},{10,... | collective-permute-start | bytes 98312 | tf_op jit(solution)/shard_map/ppermute | solution.py:21
  174.4 4.8 %collective-permute-start.31 = (f32[64,128]{1,0:T(8,128)S(1)}, f32[64,128]{1,0:T(8,128)S(1)}, u32[]{:S(2)}, u32[]{:S(2)}) collective-permute-start(f32[64,128]{1,0:T(8,128)S(1)} %add_add_fusion.2), channel_id=1, source_target_pairs={{0,2},{1,3},{2,0},{3,1},{4,6},{5,7},{6,4},{7,5},{8,10},{9,11},{10,... | collective-permute-start | bytes 98312 | tf_op jit(solution)/shard_map/ppermute | solution.py:21
  175.5 4.0 %collective-permute-start.30 = (f32[64,128]{1,0:T(8,128)S(1)}, f32[64,128]{1,0:T(8,128)S(1)}, u32[]{:S(2)}, u32[]{:S(2)}) collective-permute-start(f32[64,128]{1,0:T(8,128)S(1)} %add_add_fusion.2), channel_id=1, source_target_pairs={{0,1},{1,0},{2,3},{3,2},{4,5},{5,4},{6,7},{7,6},{8,9},{9,8},{10,11... | collective-permute-start | bytes 98312 | tf_op jit(solution)/shard_map/ppermute | solution.py:21
  188.4 13.6 %collective-permute-start.34 = (f32[16,32,128]{2,1,0:T(8,128)}, f32[16,32,128]{2,1,0:T(8,128)S(1)}, u32[]{:S(2)}, u32[]{:S(2)}) collective-permute-start(f32[16,32,128]{2,1,0:T(8,128)} %get-tuple-element.76), channel_id=1, source_target_pairs={{0,1},{1,0},{2,3},{3,2},{4,5},{5,4},{6,7},{7,6},{8,9},{9,8},{10,11... | collective-permute-start | bytes 786440 | tf_op jit(solution)/shard_map/ppermute | solution.py:21
  189.2 21.5 %collective-permute-start.35 = (f32[16,32,128]{2,1,0:T(8,128)}, f32[16,32,128]{2,1,0:T(8,128)S(1)}, u32[]{:S(2)}, u32[]{:S(2)}) collective-permute-start(f32[16,32,128]{2,1,0:T(8,128)} %get-tuple-element.77), channel_id=1, source_target_pairs={{0,2},{1,3},{2,0},{3,1},{4,6},{5,7},{6,4},{7,5},{8,10},{9,11},{10,... | collective-permute-start | bytes 786440 | tf_op jit(solution)/shard_map/ppermute | solution.py:21
  191.2 19.5 %collective-permute-start.36 = (f32[16,32,128]{2,1,0:T(8,128)}, f32[16,32,128]{2,1,0:T(8,128)S(1)}, u32[]{:S(2)}, u32[]{:S(2)}) collective-permute-start(f32[16,32,128]{2,1,0:T(8,128)} %get-tuple-element.78), channel_id=1, source_target_pairs={{0,3},{1,2},{2,1},{3,0},{4,7},{5,6},{6,5},{7,4},{8,11},{9,10},{10,... | collective-permute-start | bytes 786440 | tf_op jit(solution)/shard_map/ppermute | solution.py:21
  (37 other events, 272.4 us)

commit v3 on v2

--- a/solution.py
+++ b/solution.py
@@ -486,14 +486,12 @@
         scratch=[(count, 2 * count), (count, count)],
     )
     outs = exchanged(list(outs))
-    basis = pl.pallas_call(
+    (basis,) = call(
         lambda *refs: place_kernel(*refs, near_share=near_share, far_share=far_share, near_rows=near_rows),
-        grid=(own_count // TILE,),
-        in_specs=[smem()] + [pl.BlockSpec((near_share + far_share, TILE, nx), lambda g: (0, g, 0))] * parts,
-        out_specs=pl.BlockSpec((TILE * rows, nx), lambda g: (g, 0)),
-        out_shape=jax.ShapeDtypeStruct((own_count * rows, nx), F32),
-        name="place",
-    )(place, *outs)
+        place,
+        outs,
+        [(own_count * rows, nx)],
+    )
     return basis.reshape(start_block.shape)
 
 
@@ -506,4 +504,6 @@
     )
     out_specs = P("blk", "slab", None, None)
 
-    return jax.shard_map(per_device, mesh=mesh, in_specs=in_specs, out_specs=out_specs, check_vma=False)
+    return jax.shard_map(
+        per_device, mesh=mesh, in_specs=in_specs, out_specs=out_specs, check_vma=False
+    )

time: 218 us -> 217 us (level)
    pallas_call x1 -> x0, Pallas kernels: 3.61 us -> none  [per_device(): pl.pallas_call(lambda *refs: place_kernel(*refs, near_share=near_share, f...]
    pallas_call x4 -> x5, Pallas kernels: 18.9 us -> 22.1 us  [call(): pl.pallas_call(kernel, in_specs=[smem()] + [whole(a.shape) for a in args]...]
  transfers between devices with their start and end apart: 37 -> 37, of which waited for: 19 -> 19; matrix products, arithmetic and copies ran while one was open for 0% -> 0% of each run, Pallas kernels for 10% -> 11%
where the time goes in v3:
time: 217 us; the launch traced here: 215 us
  waiting for transfers between devices  103 us (47%)
  starting transfers between devices  60 us (28%)
  Pallas kernels  44.2 us (20%)
  local copies, waits for them, and re-layouts  4.08 us (2%)
  other arithmetic  2.89 us (1%)
    ppermute x33, waiting for transfers between devices, swap(): lax.ppermute(x, axis, [(i, i ^ bits) for i in range(lax.axis_size(axis))])  103 us
    ppermute x33, starting transfers between devices, swap(): lax.ppermute(x, axis, [(i, i ^ bits) for i in range(lax.axis_size(axis))])  49.1 us
    pallas_call x5, Pallas kernels, call(): pl.pallas_call(kernel, in_specs=[smem()] + [whole(a.shape) for a in args]...  22.1 us
    pallas_call x1, Pallas kernels, filtered_rows(): pl.pallas_call(lambda *refs: filter_kernel(*refs, steps=DEGREE, ny=ny), g...  12.4 us
    pallas_call x3, Pallas kernels, split_modes(): pl.pallas_call(lambda *refs: kernel(*refs, total=total), grid=(outs[0][1]...  9.69 us
  transfers between devices with their start and end apart: 37, of which 19 were waited for; matrix products, arithmetic and copies ran while one was open for 0% of the time, Pallas kernels for 11%

profile of v3, /device:TPU:0, one launch (start us, length us, event | category | flops | bytes accessed | tf_op | source)
XLA Modules:
  0.0 214.7 jit_solution(6037341616221783311)
XLA Ops:
  0.6 3.1 %shard_map.47 = (f32[12,96,128]{2,1,0:T(8,128)}, f32[12,96,128]{2,1,0:T(8,128)}) custom-call(s32[2]{0:T(128)} %pad_add_fusion.refs_0_, f32[6144,128]{1,0:T(8,128)} %bitcast.7), custom_call_target="tpu_custom_call" | custom-call | tf_op jit(solution)/shard_map/pallas_call | solution.py:93
  5.1 4.1 %collective-permute-start = (f32[32,8,8,128]{3,2,1,0:T(8,128)S(1)}, f32[32,8,8,128]{3,2,1,0:T(8,128)}, u32[]{:S(2)}, u32[]{:S(2)}) collective-permute-start(f32[32,8,8,128]{3,2,1,0:T(8,128)S(1)} %copy-done.3), channel_id=1, source_target_pairs={{0,4},{4,8},{8,12},{12,16},{16,20},{20,24},{24,28},{1,5},{5,9},{9,... | collective-permute-start | bytes 3145736 | tf_op jit(solution)/shard_map/ppermute | solution.py:200
  11.2 4.1 %collective-permute-start.2 = (f32[8,8,128]{2,1,0:T(8,128)S(1)}, f32[8,8,128]{2,1,0:T(8,128)S(1)}, u32[]{:S(2)}, u32[]{:S(2)}) collective-permute-start(f32[8,8,128]{2,1,0:T(8,128)S(1)} %select_multiply_fusion.refs_4_), channel_id=1, source_target_pairs={{0,4},{4,8},{8,12},{12,16},{16,20},{20,24},{24,28},{1,5},{5,9},{9,... | collective-permute-start | bytes 98312 | tf_op jit(solution)/shard_map/ppermute | solution.py:202
  15.4 2.8 %shard_map.48 = f32[12,96,128]{2,1,0:T(8,128)} custom-call(s32[2]{0:T(128)} %pad_add_fusion.refs_0_, f32[6144,128]{1,0:T(8,128)} %bitcast.8), custom_call_target="tpu_custom_call" | custom-call | tf_op jit(solution)/shard_map/pallas_call | solution.py:93
  18.2 3.0 %collective-permute-start.8 = (f32[12,96,128]{2,1,0:T(8,128)}, f32[12,96,128]{2,1,0:T(8,128)S(1)}, u32[]{:S(2)}, u32[]{:S(2)}) collective-permute-start(f32[12,96,128]{2,1,0:T(8,128)} %shard_map.48), channel_id=1, source_target_pairs={{0,2},{1,3},{2,0},{3,1},{4,6},{5,7},{6,4},{7,5},{8,10},{9,11},{10,... | collective-permute-start | bytes 1769480 | tf_op jit(solution)/shard_map/ppermute | solution.py:21
  23.4 12.4 %chebyshev.1 = (f32[12,32,128]{2,1,0:T(8,128)}, f32[12,32,128]{2,1,0:T(8,128)}, f32[12,32,128]{2,1,0:T(8,128)}, f32[12,32,128]{2,1,0:T(8,128)}, f32[16,32,128]{2,1,0:T(8,128)}) custom-call(s32[2]{0:T(128)} %pad_add_fusion.refs_0_, f32[2048,128]{1,0:T(8,128)} %bitcast.10, f32[2048,128]{1,0:T(8,128)} %bitcast.4.refs_2_, f32[2048,128]{1,0:T(8,128)} %bitcast.5.refs_3_, ...), custom_call_target="tpu_custom_call" | custom-call | tf_op jit(solution)/shard_map/chebyshev/pallas_call | solution.py:206
  37.2 2.5 %collective-permute-start.4 = (f32[16,32,128]{2,1,0:T(8,128)}, f32[16,32,128]{2,1,0:T(8,128)S(1)}, u32[]{:S(2)}, u32[]{:S(2)}) collective-permute-start(f32[16,32,128]{2,1,0:T(8,128)} %get-tuple-element.50.refs_2_), channel_id=1, source_target_pairs={{0,1},{1,0},{2,3},{3,2},{4,5},{5,4},{6,7},{7,6},{8,9},{9,8},{10,11... | collective-permute-start | bytes 786440 | tf_op jit(solution)/shard_map/ppermute | solution.py:21
  39.7 44.3 %collective-permute-done.5.refs_4_ = f32[16,32,128]{2,1,0:T(8,128)S(1)} collective-permute-done((f32[16,32,128]{2,1,0:T(8,128)}, f32[16,32,128]{2,1,0:T(8,128)S(1)}, u32[]{:S(2)}, u32[]{:S(2)}) %collective-permute-start.5) | collective-permute-done | bytes 262176 | tf_op jit(solution)/shard_map/ppermute | solution.py:21
  84.0 1.8 collective-permute-start.6
  86.0 3.1 %collective-permute-start.11 = (f32[12,32,128]{2,1,0:T(8,128)}, f32[12,32,128]{2,1,0:T(8,128)S(1)}, u32[]{:S(2)}, u32[]{:S(2)}) collective-permute-start(f32[12,32,128]{2,1,0:T(8,128)} %get-tuple-element.59), channel_id=1, source_target_pairs={{0,2},{1,3},{2,0},{3,1},{4,6},{5,7},{6,4},{7,5},{8,10},{9,11},{10,... | collective-permute-start | bytes 589832 | tf_op jit(solution)/shard_map/ppermute | solution.py:21
  90.7 3.8 %shard_map.46 = (f32[12,96,128]{2,1,0:T(8,128)}, f32[16,96,128]{2,1,0:T(8,128)}, f32[4,96,128]{2,1,0:T(8,128)}, f32[4,96,128]{2,1,0:T(8,128)}, f32[4,96,128]{2,1,0:T(8,128)}, /*index=5*/f32[4,96,128]{2,1,0:T(8,128)}) custom-call(s32[2]{0:T(128)} %pad_add_fusion.refs_0_, f32[6144,128]{1,0:T(8,128)} %bitcast.9), custom_call_target="tpu_custom_call" | custom-call | tf_op jit(solution)/shard_map/pallas_call | solution.py:93
  94.4 6.8 %collective-permute-done.10.refs_6_ = f32[12,32,128]{2,1,0:T(8,128)S(1)} collective-permute-done((f32[12,32,128]{2,1,0:T(8,128)}, f32[12,32,128]{2,1,0:T(8,128)S(1)}, u32[]{:S(2)}, u32[]{:S(2)}) %collective-permute-start.10) | collective-permute-done | bytes 196640 | tf_op jit(solution)/shard_map/ppermute | solution.py:21
  101.2 6.5 %collective-permute-done.12.refs_8_ = f32[12,32,128]{2,1,0:T(8,128)S(1)} collective-permute-done((f32[12,32,128]{2,1,0:T(8,128)}, f32[12,32,128]{2,1,0:T(8,128)S(1)}, u32[]{:S(2)}, u32[]{:S(2)}) %collective-permute-start.12) | collective-permute-done | bytes 196640 | tf_op jit(solution)/shard_map/ppermute | solution.py:21
  108.4 3.6 %shard_map.49 = (f32[12,128,128]{2,1,0:T(8,128)}, f32[96,128]{1,0:T(8,128)}, f32[96,128]{1,0:T(8,128)}, f32[96,128]{1,0:T(8,128)}, f32[96,128]{1,0:T(8,128)}) custom-call(s32[2]{0:T(128)} %pad_add_fusion.refs_0_, f32[12,96,128]{2,1,0:T(8,128)} %get-tuple-element.54.refs_1_.refs_5_, f32[12,96,128]{2,1,0:T(8,128)} %copy-done.1, f32[12,96,128]{2,1,0:T(8,128)} %copy-done, ...), custom_call_target="tpu_custom_call" | custom-call | tf_op jit(solution)/shard_map/pallas_call | solution.py:33
  112.3 2.2 %collective-permute-start.14 = (f32[96,128]{1,0:T(8,128)}, f32[96,128]{1,0:T(8,128)S(1)}, u32[]{:S(2)}, u32[]{:S(2)}) collective-permute-start(f32[96,128]{1,0:T(8,128)} %get-tuple-element.63), channel_id=1, source_target_pairs={{0,2},{1,3},{2,0},{3,1},{4,6},{5,7},{6,4},{7,5},{8,10},{9,11},{10,... | collective-permute-start | bytes 147464 | tf_op jit(solution)/shard_map/ppermute | solution.py:21
  114.5 2.0 collective-permute-start.15
  116.5 2.6 %collective-permute-done.14.refs_8_ = f32[96,128]{1,0:T(8,128)S(1)} collective-permute-done((f32[96,128]{1,0:T(8,128)}, f32[96,128]{1,0:T(8,128)S(1)}, u32[]{:S(2)}, u32[]{:S(2)}) %collective-permute-start.14) | collective-permute-done | bytes 49184 | tf_op jit(solution)/shard_map/ppermute | solution.py:21
  121.2 2.8 %shard_map.50 = (f32[16,128,128]{2,1,0:T(8,128)}, f32[96,128]{1,0:T(8,128)}) custom-call(s32[2]{0:T(128)} %pad_add_fusion.refs_0_, f32[16,96,128]{2,1,0:T(8,128)} %get-tuple-element.42.refs_1_, f32[16,32,128]{2,1,0:T(8,128)} %get-tuple-element.50.refs_2_, f32[16,32,128]{2,1,0:T(8,128)} %copy-done.5, f32[16,32,128]{2,1,0:T(8,128)} %copy-done.4, ...), custom_call_target="tpu_custom_call" | custom-call | tf_op jit(solution)/shard_map/pallas_call | solution.py:33
  127.1 2.6 %collective-permute-start.18 = (f32[96,128]{1,0:T(8,128)S(1)}, f32[96,128]{1,0:T(8,128)S(1)}, u32[]{:S(2)}, u32[]{:S(2)}) collective-permute-start(f32[96,128]{1,0:T(8,128)S(1)} %add.38), channel_id=1, source_target_pairs={{0,16},{4,20},{8,24},{12,28},{16,0},{20,4},{24,8},{28,12},{1,17},{... | collective-permute-start | bytes 147464 | tf_op jit(solution)/shard_map/ppermute | solution.py:21
  129.8 2.6 %collective-permute-start.24 = (f32[4,96,128]{2,1,0:T(8,128)}, f32[4,96,128]{2,1,0:T(8,128)S(1)}, u32[]{:S(2)}, u32[]{:S(2)}) collective-permute-start(f32[4,96,128]{2,1,0:T(8,128)} %get-tuple-element.68), channel_id=1, source_target_pairs={{0,2},{1,3},{2,0},{3,1},{4,6},{5,7},{6,4},{7,5},{8,10},{9,11},{10,... | collective-permute-start | bytes 589832 | tf_op jit(solution)/shard_map/ppermute | solution.py:21
  132.4 1.8 collective-permute-start.25
  134.2 2.1 collective-permute-start.22
  136.3 10.7 %collective-permute-done.22.refs_4_ = f32[96,128]{1,0:T(8,128)S(1)} collective-permute-done((f32[96,128]{1,0:T(8,128)S(1)}, f32[96,128]{1,0:T(8,128)S(1)}, u32[]{:S(2)}, u32[]{:S(2)}) %collective-permute-start.22) | collective-permute-done | bytes 49184 | tf_op jit(solution)/shard_map/ppermute | solution.py:21
  147.0 7.1 %collective-permute-start.20 = (f32[96,128]{1,0:T(8,128)S(1)}, f32[96,128]{1,0:T(8,128)S(1)}, u32[]{:S(2)}, u32[]{:S(2)}) collective-permute-start(f32[96,128]{1,0:T(8,128)S(1)} %add_add_fusion.refs_1_), channel_id=1, source_target_pairs={{0,1},{1,0},{2,3},{3,2},{4,5},{5,4},{6,7},{7,6},{8,9},{9,8},{10,11... | collective-permute-start | bytes 147464 | tf_op jit(solution)/shard_map/ppermute | solution.py:21
  154.2 2.0 collective-permute-done.20.refs_2_
  157.1 5.6 %shard_map.51 = (f32[128,2048]{1,0:T(8,128)}, f32[64,128]{1,0:T(8,128)}, f32[64,128]{1,0:T(8,128)}) custom-call(s32[2]{0:T(128)} %pad_add_fusion.refs_0_, f32[96,128]{1,0:T(8,128)} %copy-done.10, f32[96,128]{1,0:T(8,128)} %copy-done.21, f32[96,128]{1,0:T(8,128)} %copy-done.20, f32[96,128]{1,0:T(8,128)} %copy-done.19, ...), custom_call_target="tpu_custom_call" | custom-call | tf_op jit(solution)/shard_map/pallas_call | solution.py:33
  172.0 2.4 %collective-permute-start.32 = (f32[64,128]{1,0:T(8,128)S(1)}, f32[64,128]{1,0:T(8,128)S(1)}, u32[]{:S(2)}, u32[]{:S(2)}) collective-permute-start(f32[64,128]{1,0:T(8,128)S(1)} %add_add_fusion.2), channel_id=1, source_target_pairs={{0,3},{1,2},{2,1},{3,0},{4,7},{5,6},{6,5},{7,4},{8,11},{9,10},{10,... | collective-permute-start | bytes 98312 | tf_op jit(solution)/shard_map/ppermute | solution.py:21
  181.5 6.9 %shard_map.52 = (f32[16,32,128]{2,1,0:T(8,128)}, f32[16,32,128]{2,1,0:T(8,128)}, f32[16,32,128]{2,1,0:T(8,128)}, f32[16,32,128]{2,1,0:T(8,128)}) custom-call(s32[2]{0:T(128)} %pad_add_fusion.refs_0_, f32[64,128]{1,0:T(8,128)} %copy-done.18, f32[64,128]{1,0:T(8,128)} %copy-done.27, f32[128,2048]{1,0:T(8,128)} %get-tuple-element.74.refs_3_), custom_call_target="tpu_custom_call" | custom-call | tf_op jit(solution)/shard_map/pallas_call | solution.py:33
  189.2 2.0 collective-permute-start.35
  192.8 9.2 %collective-permute-done.34.refs_2_ = f32[16,32,128]{2,1,0:T(8,128)S(1)} collective-permute-done((f32[16,32,128]{2,1,0:T(8,128)}, f32[16,32,128]{2,1,0:T(8,128)S(1)}, u32[]{:S(2)}, u32[]{:S(2)}) %collective-permute-start.34) | collective-permute-done | bytes 262176 | tf_op jit(solution)/shard_map/ppermute | solution.py:21
  202.0 8.8 %collective-permute-done.35.refs_3_ = f32[16,32,128]{2,1,0:T(8,128)S(1)} collective-permute-done((f32[16,32,128]{2,1,0:T(8,128)}, f32[16,32,128]{2,1,0:T(8,128)S(1)}, u32[]{:S(2)}, u32[]{:S(2)}) %collective-permute-start.35) | collective-permute-done | bytes 262176 | tf_op jit(solution)/shard_map/ppermute | solution.py:21
  211.5 3.1 %shard_map.53 = f32[2048,128]{1,0:T(8,128)} custom-call(s32[2]{0:T(128)} %pad_add_fusion.refs_0_, f32[16,32,128]{2,1,0:T(8,128)} %get-tuple-element.75.refs_1_, f32[16,32,128]{2,1,0:T(8,128)} %copy-done.7, f32[16,32,128]{2,1,0:T(8,128)} %copy-done.8, f32[16,32,128]{2,1,0:T(8,128)} %copy-done.9), custom_call_target="tpu_custom_call" | custom-call | tf_op jit(solution)/shard_map/pallas_call | solution.py:33
  (124 shorter events, 35.9 us)
Async XLA Ops:
  3.7 19.1 %collective-permute-start.1 = (f32[32,8,8,128]{3,2,1,0:T(8,128)S(1)}, f32[32,8,8,128]{3,2,1,0:T(8,128)}, u32[]{:S(2)}, u32[]{:S(2)}) collective-permute-start(f32[32,8,8,128]{3,2,1,0:T(8,128)S(1)} %copy-done.3), channel_id=1, source_target_pairs={{4,0},{8,4},{12,8},{16,12},{20,16},{24,20},{28,24},{5,1},{9,5},{13... | collective-permute-start | bytes 3145736 | tf_op jit(solution)/shard_map/ppermute | solution.py:201
  5.1 17.7 %collective-permute-start = (f32[32,8,8,128]{3,2,1,0:T(8,128)S(1)}, f32[32,8,8,128]{3,2,1,0:T(8,128)}, u32[]{:S(2)}, u32[]{:S(2)}) collective-permute-start(f32[32,8,8,128]{3,2,1,0:T(8,128)S(1)} %copy-done.3), channel_id=1, source_target_pairs={{0,4},{4,8},{8,12},{12,16},{16,20},{20,24},{24,28},{1,5},{5,9},{9,... | collective-permute-start | bytes 3145736 | tf_op jit(solution)/shard_map/ppermute | solution.py:200
  9.9 11.3 %collective-permute-start.3 = (f32[8,8,128]{2,1,0:T(8,128)S(1)}, f32[8,8,128]{2,1,0:T(8,128)S(1)}, u32[]{:S(2)}, u32[]{:S(2)}) collective-permute-start(f32[8,8,128]{2,1,0:T(8,128)S(1)} %select_multiply_fusion.refs_4_), channel_id=1, source_target_pairs={{4,0},{8,4},{12,8},{16,12},{20,16},{24,20},{28,24},{5,1},{9,5},{13... | collective-permute-start | bytes 98312 | tf_op jit(solution)/shard_map/ppermute | solution.py:203
  11.2 11.6 %collective-permute-start.2 = (f32[8,8,128]{2,1,0:T(8,128)S(1)}, f32[8,8,128]{2,1,0:T(8,128)S(1)}, u32[]{:S(2)}, u32[]{:S(2)}) collective-permute-start(f32[8,8,128]{2,1,0:T(8,128)S(1)} %select_multiply_fusion.refs_4_), channel_id=1, source_target_pairs={{0,4},{4,8},{8,12},{12,16},{16,20},{20,24},{24,28},{1,5},{5,9},{9,... | collective-permute-start | bytes 98312 | tf_op jit(solution)/shard_map/ppermute | solution.py:202
  18.2 67.6 %collective-permute-start.8 = (f32[12,96,128]{2,1,0:T(8,128)}, f32[12,96,128]{2,1,0:T(8,128)S(1)}, u32[]{:S(2)}, u32[]{:S(2)}) collective-permute-start(f32[12,96,128]{2,1,0:T(8,128)} %shard_map.48), channel_id=1, source_target_pairs={{0,2},{1,3},{2,0},{3,1},{4,6},{5,7},{6,4},{7,5},{8,10},{9,11},{10,... | collective-permute-start | bytes 1769480 | tf_op jit(solution)/shard_map/ppermute | solution.py:21
  21.2 64.9 %collective-permute-start.7 = (f32[12,96,128]{2,1,0:T(8,128)S(1)}, f32[12,96,128]{2,1,0:T(8,128)S(1)}, u32[]{:S(2)}, u32[]{:S(2)}) collective-permute-start(f32[12,96,128]{2,1,0:T(8,128)S(1)} %copy-done.30), channel_id=1, source_target_pairs={{0,1},{1,0},{2,3},{3,2},{4,5},{5,4},{6,7},{7,6},{8,9},{9,8},{10,11... | collective-permute-start | bytes 1769480 | tf_op jit(solution)/shard_map/ppermute | solution.py:21
  22.8 66.4 %collective-permute-start.9 = (f32[12,96,128]{2,1,0:T(8,128)}, f32[12,96,128]{2,1,0:T(8,128)S(1)}, u32[]{:S(2)}, u32[]{:S(2)}) collective-permute-start(f32[12,96,128]{2,1,0:T(8,128)} %get-tuple-element.56), channel_id=1, source_target_pairs={{0,3},{1,2},{2,1},{3,0},{4,7},{5,6},{6,5},{7,4},{8,11},{9,10},{10,... | collective-permute-start | bytes 1769480 | tf_op jit(solution)/shard_map/ppermute | solution.py:21
  35.8 48.2 %collective-permute-start.5 = (f32[16,32,128]{2,1,0:T(8,128)}, f32[16,32,128]{2,1,0:T(8,128)S(1)}, u32[]{:S(2)}, u32[]{:S(2)}) collective-permute-start(f32[16,32,128]{2,1,0:T(8,128)} %get-tuple-element.50.refs_2_), channel_id=1, source_target_pairs={{0,2},{1,3},{2,0},{3,1},{4,6},{5,7},{6,4},{7,5},{8,10},{9,11},{10,... | collective-permute-start | bytes 786440 | tf_op jit(solution)/shard_map/ppermute | solution.py:21
  37.2 79.2 %collective-permute-start.4 = (f32[16,32,128]{2,1,0:T(8,128)}, f32[16,32,128]{2,1,0:T(8,128)S(1)}, u32[]{:S(2)}, u32[]{:S(2)}) collective-permute-start(f32[16,32,128]{2,1,0:T(8,128)} %get-tuple-element.50.refs_2_), channel_id=1, source_target_pairs={{0,1},{1,0},{2,3},{3,2},{4,5},{5,4},{6,7},{7,6},{8,9},{9,8},{10,11... | collective-permute-start | bytes 786440 | tf_op jit(solution)/shard_map/ppermute | solution.py:21
  84.0 32.5 %collective-permute-start.6 = (f32[16,32,128]{2,1,0:T(8,128)S(1)}, f32[16,32,128]{2,1,0:T(8,128)S(1)}, u32[]{:S(2)}, u32[]{:S(2)}) collective-permute-start(f32[16,32,128]{2,1,0:T(8,128)S(1)} %collective-permute-done.5.refs_4_), channel_id=1, source_target_pairs={{0,1},{1,0},{2,3},{3,2},{4,5},{5,4},{6,7},{7,6},{8,9},{9,8},{10,11... | collective-permute-start | bytes 786440 | tf_op jit(solution)/shard_map/ppermute | solution.py:21
  85.8 15.4 %collective-permute-start.10 = (f32[12,32,128]{2,1,0:T(8,128)}, f32[12,32,128]{2,1,0:T(8,128)S(1)}, u32[]{:S(2)}, u32[]{:S(2)}) collective-permute-start(f32[12,32,128]{2,1,0:T(8,128)} %get-tuple-element.58), channel_id=1, source_target_pairs={{0,1},{1,0},{2,3},{3,2},{4,5},{5,4},{6,7},{7,6},{8,9},{9,8},{10,11... | collective-permute-start | bytes 589832 | tf_op jit(solution)/shard_map/ppermute | solution.py:21
  86.0 15.2 %collective-permute-start.11 = (f32[12,32,128]{2,1,0:T(8,128)}, f32[12,32,128]{2,1,0:T(8,128)S(1)}, u32[]{:S(2)}, u32[]{:S(2)}) collective-permute-start(f32[12,32,128]{2,1,0:T(8,128)} %get-tuple-element.59), channel_id=1, source_target_pairs={{0,2},{1,3},{2,0},{3,1},{4,6},{5,7},{6,4},{7,5},{8,10},{9,11},{10,... | collective-permute-start | bytes 589832 | tf_op jit(solution)/shard_map/ppermute | solution.py:21
  89.2 18.6 %collective-permute-start.12 = (f32[12,32,128]{2,1,0:T(8,128)}, f32[12,32,128]{2,1,0:T(8,128)S(1)}, u32[]{:S(2)}, u32[]{:S(2)}) collective-permute-start(f32[12,32,128]{2,1,0:T(8,128)} %get-tuple-element.60), channel_id=1, source_target_pairs={{0,3},{1,2},{2,1},{3,0},{4,7},{5,6},{6,5},{7,4},{8,11},{9,10},{10,... | collective-permute-start | bytes 589832 | tf_op jit(solution)/shard_map/ppermute | solution.py:21
  112.0 4.4 %collective-permute-start.13 = (f32[96,128]{1,0:T(8,128)}, f32[96,128]{1,0:T(8,128)S(1)}, u32[]{:S(2)}, u32[]{:S(2)}) collective-permute-start(f32[96,128]{1,0:T(8,128)} %get-tuple-element.62), channel_id=1, source_target_pairs={{0,1},{1,0},{2,3},{3,2},{4,5},{5,4},{6,7},{7,6},{8,9},{9,8},{10,11... | collective-permute-start | bytes 147464 | tf_op jit(solution)/shard_map/ppermute | solution.py:21
  112.3 6.8 %collective-permute-start.14 = (f32[96,128]{1,0:T(8,128)}, f32[96,128]{1,0:T(8,128)S(1)}, u32[]{:S(2)}, u32[]{:S(2)}) collective-permute-start(f32[96,128]{1,0:T(8,128)} %get-tuple-element.63), channel_id=1, source_target_pairs={{0,2},{1,3},{2,0},{3,1},{4,6},{5,7},{6,4},{7,5},{8,10},{9,11},{10,... | collective-permute-start | bytes 147464 | tf_op jit(solution)/shard_map/ppermute | solution.py:21
  114.5 6.1 %collective-permute-start.15 = (f32[96,128]{1,0:T(8,128)}, f32[96,128]{1,0:T(8,128)S(1)}, u32[]{:S(2)}, u32[]{:S(2)}) collective-permute-start(f32[96,128]{1,0:T(8,128)} %get-tuple-element.64), channel_id=1, source_target_pairs={{0,3},{1,2},{2,1},{3,0},{4,7},{5,6},{6,5},{7,4},{8,11},{9,10},{10,... | collective-permute-start | bytes 147464 | tf_op jit(solution)/shard_map/ppermute | solution.py:21
  126.3 6.1 %collective-permute-start.19 = (f32[96,128]{1,0:T(8,128)S(1)}, f32[96,128]{1,0:T(8,128)S(1)}, u32[]{:S(2)}, u32[]{:S(2)}) collective-permute-start(f32[96,128]{1,0:T(8,128)S(1)} %add.38), channel_id=1, source_target_pairs={{0,24},{4,28},{8,16},{12,20},{16,8},{20,12},{24,0},{28,4},{1,25},{... | collective-permute-start | bytes 147464 | tf_op jit(solution)/shard_map/ppermute | solution.py:21
  127.1 7.1 %collective-permute-start.18 = (f32[96,128]{1,0:T(8,128)S(1)}, f32[96,128]{1,0:T(8,128)S(1)}, u32[]{:S(2)}, u32[]{:S(2)}) collective-permute-start(f32[96,128]{1,0:T(8,128)S(1)} %add.38), channel_id=1, source_target_pairs={{0,16},{4,20},{8,24},{12,28},{16,0},{20,4},{24,8},{28,12},{1,17},{... | collective-permute-start | bytes 147464 | tf_op jit(solution)/shard_map/ppermute | solution.py:21
  129.7 4.5 %collective-permute-start.17 = (f32[96,128]{1,0:T(8,128)S(1)}, f32[96,128]{1,0:T(8,128)S(1)}, u32[]{:S(2)}, u32[]{:S(2)}) collective-permute-start(f32[96,128]{1,0:T(8,128)S(1)} %add.38), channel_id=1, source_target_pairs={{0,8},{4,12},{8,0},{12,4},{16,24},{20,28},{24,16},{28,20},{1,9},{5... | collective-permute-start | bytes 147464 | tf_op jit(solution)/shard_map/ppermute | solution.py:21
  129.8 26.4 %collective-permute-start.23 = (f32[4,96,128]{2,1,0:T(8,128)}, f32[4,96,128]{2,1,0:T(8,128)S(1)}, u32[]{:S(2)}, u32[]{:S(2)}) collective-permute-start(f32[4,96,128]{2,1,0:T(8,128)} %get-tuple-element.67), channel_id=1, source_target_pairs={{0,1},{1,0},{2,3},{3,2},{4,5},{5,4},{6,7},{7,6},{8,9},{9,8},{10,11... | collective-permute-start | bytes 589832 | tf_op jit(solution)/shard_map/ppermute | solution.py:21
  129.8 26.4 %collective-permute-start.24 = (f32[4,96,128]{2,1,0:T(8,128)}, f32[4,96,128]{2,1,0:T(8,128)S(1)}, u32[]{:S(2)}, u32[]{:S(2)}) collective-permute-start(f32[4,96,128]{2,1,0:T(8,128)} %get-tuple-element.68), channel_id=1, source_target_pairs={{0,2},{1,3},{2,0},{3,1},{4,6},{5,7},{6,4},{7,5},{8,10},{9,11},{10,... | collective-permute-start | bytes 589832 | tf_op jit(solution)/shard_map/ppermute | solution.py:21
  132.4 23.8 %collective-permute-start.25 = (f32[4,96,128]{2,1,0:T(8,128)S(1)}, f32[4,96,128]{2,1,0:T(8,128)S(1)}, u32[]{:S(2)}, u32[]{:S(2)}) collective-permute-start(f32[4,96,128]{2,1,0:T(8,128)S(1)} %copy-done.31), channel_id=1, source_target_pairs={{0,3},{1,2},{2,1},{3,0},{4,7},{5,6},{6,5},{7,4},{8,11},{9,10},{10,... | collective-permute-start | bytes 589832 | tf_op jit(solution)/shard_map/ppermute | solution.py:21
  134.2 12.8 %collective-permute-start.22 = (f32[96,128]{1,0:T(8,128)S(1)}, f32[96,128]{1,0:T(8,128)S(1)}, u32[]{:S(2)}, u32[]{:S(2)}) collective-permute-start(f32[96,128]{1,0:T(8,128)S(1)} %add_add_fusion.refs_1_), channel_id=1, source_target_pairs={{0,3},{1,2},{2,1},{3,0},{4,7},{5,6},{6,5},{7,4},{8,11},{9,10},{10,... | collective-permute-start | bytes 147464 | tf_op jit(solution)/shard_map/ppermute | solution.py:21
  136.3 17.9 %collective-permute-start.21 = (f32[96,128]{1,0:T(8,128)S(1)}, f32[96,128]{1,0:T(8,128)S(1)}, u32[]{:S(2)}, u32[]{:S(2)}) collective-permute-start(f32[96,128]{1,0:T(8,128)S(1)} %add_add_fusion.refs_1_), channel_id=1, source_target_pairs={{0,2},{1,3},{2,0},{3,1},{4,6},{5,7},{6,4},{7,5},{8,10},{9,11},{10,... | collective-permute-start | bytes 147464 | tf_op jit(solution)/shard_map/ppermute | solution.py:21
  147.0 9.2 %collective-permute-start.20 = (f32[96,128]{1,0:T(8,128)S(1)}, f32[96,128]{1,0:T(8,128)S(1)}, u32[]{:S(2)}, u32[]{:S(2)}) collective-permute-start(f32[96,128]{1,0:T(8,128)S(1)} %add_add_fusion.refs_1_), channel_id=1, source_target_pairs={{0,1},{1,0},{2,3},{3,2},{4,5},{5,4},{6,7},{7,6},{8,9},{9,8},{10,11... | collective-permute-start | bytes 147464 | tf_op jit(solution)/shard_map/ppermute | solution.py:21
  164.8 4.8 %collective-permute-start.29 = (f32[64,128]{1,0:T(8,128)S(1)}, f32[64,128]{1,0:T(8,128)S(1)}, u32[]{:S(2)}, u32[]{:S(2)}) collective-permute-start(f32[64,128]{1,0:T(8,128)S(1)} %add.42), channel_id=1, source_target_pairs={{0,24},{4,28},{8,16},{12,20},{16,8},{20,12},{24,0},{28,4},{1,25},{... | collective-permute-start | bytes 98312 | tf_op jit(solution)/shard_map/ppermute | solution.py:21
  172.0 6.0 %collective-permute-start.32 = (f32[64,128]{1,0:T(8,128)S(1)}, f32[64,128]{1,0:T(8,128)S(1)}, u32[]{:S(2)}, u32[]{:S(2)}) collective-permute-start(f32[64,128]{1,0:T(8,128)S(1)} %add_add_fusion.2), channel_id=1, source_target_pairs={{0,3},{1,2},{2,1},{3,0},{4,7},{5,6},{6,5},{7,4},{8,11},{9,10},{10,... | collective-permute-start | bytes 98312 | tf_op jit(solution)/shard_map/ppermute | solution.py:21
  174.4 4.8 %collective-permute-start.31 = (f32[64,128]{1,0:T(8,128)S(1)}, f32[64,128]{1,0:T(8,128)S(1)}, u32[]{:S(2)}, u32[]{:S(2)}) collective-permute-start(f32[64,128]{1,0:T(8,128)S(1)} %add_add_fusion.2), channel_id=1, source_target_pairs={{0,2},{1,3},{2,0},{3,1},{4,6},{5,7},{6,4},{7,5},{8,10},{9,11},{10,... | collective-permute-start | bytes 98312 | tf_op jit(solution)/shard_map/ppermute | solution.py:21
  175.5 4.0 %collective-permute-start.30 = (f32[64,128]{1,0:T(8,128)S(1)}, f32[64,128]{1,0:T(8,128)S(1)}, u32[]{:S(2)}, u32[]{:S(2)}) collective-permute-start(f32[64,128]{1,0:T(8,128)S(1)} %add_add_fusion.2), channel_id=1, source_target_pairs={{0,1},{1,0},{2,3},{3,2},{4,5},{5,4},{6,7},{7,6},{8,9},{9,8},{10,11... | collective-permute-start | bytes 98312 | tf_op jit(solution)/shard_map/ppermute | solution.py:21
  188.4 13.6 %collective-permute-start.34 = (f32[16,32,128]{2,1,0:T(8,128)}, f32[16,32,128]{2,1,0:T(8,128)S(1)}, u32[]{:S(2)}, u32[]{:S(2)}) collective-permute-start(f32[16,32,128]{2,1,0:T(8,128)} %get-tuple-element.76), channel_id=1, source_target_pairs={{0,1},{1,0},{2,3},{3,2},{4,5},{5,4},{6,7},{7,6},{8,9},{9,8},{10,11... | collective-permute-start | bytes 786440 | tf_op jit(solution)/shard_map/ppermute | solution.py:21
  189.2 21.5 %collective-permute-start.35 = (f32[16,32,128]{2,1,0:T(8,128)}, f32[16,32,128]{2,1,0:T(8,128)S(1)}, u32[]{:S(2)}, u32[]{:S(2)}) collective-permute-start(f32[16,32,128]{2,1,0:T(8,128)} %get-tuple-element.77), channel_id=1, source_target_pairs={{0,2},{1,3},{2,0},{3,1},{4,6},{5,7},{6,4},{7,5},{8,10},{9,11},{10,... | collective-permute-start | bytes 786440 | tf_op jit(solution)/shard_map/ppermute | solution.py:21
  191.2 19.5 %collective-permute-start.36 = (f32[16,32,128]{2,1,0:T(8,128)}, f32[16,32,128]{2,1,0:T(8,128)S(1)}, u32[]{:S(2)}, u32[]{:S(2)}) collective-permute-start(f32[16,32,128]{2,1,0:T(8,128)} %get-tuple-element.78), channel_id=1, source_target_pairs={{0,3},{1,2},{2,1},{3,0},{4,7},{5,6},{6,5},{7,4},{8,11},{9,10},{10,... | collective-permute-start | bytes 786440 | tf_op jit(solution)/shard_map/ppermute | solution.py:21
  (37 other events, 272.4 us)
